TPU v7x, 32 devices: a whole 2x2x4 slice. The times are simulated.
32 devices in a mesh: shard: 4 (over y, core), ctx: 4 (over z), tensor: 2 (over x).
Axes of the slice: x: 2, y: 2, z: 4, core: 2. Of those that a mesh axis runs over, the one named last changes fastest.
Arguments:
- layer_input: bfloat16 [4, 2048, 768], P('shard', 'ctx'), may hold values from -6 to 6
- segments: int32 [4, 2048], P('shard'), may hold values from 0 to 2, as said below
- w_qkv: bfloat16 [768, 3, 768], P(('shard', 'ctx'), None, 'tensor'), may hold values from -0.21875 to 0.21875
- b_qv: bfloat16 [2, 768], P(None, 'tensor'), may hold values from -2 to 2
- w_out: bfloat16 [768, 768], P(('shard', 'ctx'), 'tensor'), may hold values from -4 to 4
- b_out: bfloat16 [768], replicated, may hold values from -2 to 2
- ln1_gain: bfloat16 [768], replicated, may hold values from 0.25 to 1.75
- ln1_bias: bfloat16 [768], replicated, may hold values from -2 to 2
- w_up: bfloat16 [768, 3072], P(('shard', 'ctx'), 'tensor'), may hold values from -0.21875 to 0.21875
- b_up: bfloat16 [3072], P('tensor'), may hold values from -2 to 2
- w_down: bfloat16 [768, 3072], P(('shard', 'ctx'), 'tensor'), may hold values from -0.109375 to 0.109375
- b_down: bfloat16 [768], replicated, may hold values from -2 to 2
- ln2_gain: bfloat16 [768], replicated, may hold values from 0.25 to 1.75
- ln2_bias: bfloat16 [768], replicated, may hold values from -2 to 2
- cotangent: bfloat16 [4, 2048, 768], P('shard', 'ctx'), may hold values from -6 to 6
Outputs:
- layer_output: bfloat16 [4, 2048, 768], P('shard', 'ctx')
- grad_input: float32 [4, 2048, 768], P('shard', 'ctx')
- grad_w_qkv: float32 [768, 3, 768], P(('shard', 'ctx'), None, 'tensor')
- grad_b_qv: float32 [2, 768], P(None, 'tensor')
- grad_w_out: float32 [768, 768], P(('shard', 'ctx'), 'tensor')
- grad_b_out: float32 [768], replicated
- grad_ln1_gain: float32 [768], replicated
- grad_ln1_bias: float32 [768], replicated
- grad_w_up: float32 [768, 3072], P(('shard', 'ctx'), 'tensor')
- grad_b_up: float32 [3072], P('tensor')
- grad_w_down: float32 [768, 3072], P(('shard', 'ctx'), 'tensor')
- grad_b_down: float32 [768], replicated
- grad_ln2_gain: float32 [768], replicated
- grad_ln2_bias: float32 [768], replicated
Inputs may be any that keep to these rules, and one draw needn't show every extreme that they name: Each packed row has exactly three segments numbered 0, 1, 2, never falling along the row; segment 1 starts within the first 512 positions and ends within the last 512 positions of the row.
All inputs are finite; a program needn't handle non-finite values.
Results may differ from a plain program's by a relative error of at most 0.02.
Values may be sent and summed in bfloat16 or wider, within the bound.
No kernel may reach another device: no remote copies, remote signals or barrier semaphores. Data moves between devices by JAX's collectives and lax.ppermute only.
A program may use at most 128 MiB of HBM per device.

v0:
```python
import jax
import jax.numpy as jnp
from jax import lax
from jax.sharding import PartitionSpec as P

HD = 64


neg_large = -1e30


def layer_norm(summed, gain, bias):
    centred = summed - jnp.mean(summed, -1, keepdims=True)
    scaling = lax.rsqrt(jnp.mean(centred * centred, -1, keepdims=True) + 1e-05)
    normal_part = centred * scaling
    return (normal_part * gain + bias, normal_part, scaling)


def norm_back(upstream, normal_part, scaling, gain):
    scaled = upstream * gain
    inner = (
        scaled
        - jnp.mean(scaled, -1, keepdims=True)
        - normal_part * jnp.mean(scaled * normal_part, -1, keepdims=True)
    )
    return (inner * scaling, jnp.sum(upstream * normal_part, 0), jnp.sum(upstream, 0))


def gelu_exact(inputs):
    return 0.5 * inputs * (1.0 + lax.erf(inputs * 0.7071067811865476))


def gelu_slope(inputs):
    return (
        0.5 * (1.0 + lax.erf(inputs * 0.7071067811865476))
        + inputs * jnp.exp(-0.5 * inputs * inputs) * 0.3989422804014327
    )


def on_device(
    layer_input,
    segments,
    w_qkv,
    b_qv,
    w_out,
    b_out,
    ln1_gain,
    ln1_bias,
    w_up,
    b_up,
    w_down,
    b_down,
    ln2_gain,
    ln2_bias,
    cotangent,
):
    inputs = layer_input[0]
    tokens = inputs.shape[0]
    group_len = tokens * lax.axis_size("ctx")
    seg_all = segments[0]
    seg_query = lax.dynamic_slice_in_dim(seg_all, lax.axis_index("ctx") * tokens, tokens)
    qkv_full, out_full, up_full, down_full = (
        lax.all_gather(w_qkv, ("shard", "ctx"), axis=0, tiled=True),
        lax.all_gather(w_out, ("shard", "ctx"), axis=0, tiled=True),
        lax.all_gather(w_up, ("shard", "ctx"), axis=0, tiled=True),
        lax.all_gather(w_down, ("shard", "ctx"), axis=0, tiled=True),
    )
    local_width = qkv_full.shape[2]
    heads_here = local_width // HD
    projected = jnp.einsum("td,dwe->wte", inputs, qkv_full, preferred_element_type=jnp.float32)
    bias_pair = b_qv.astype(jnp.float32)
    queries = (projected[0] + bias_pair[0]).astype(jnp.bfloat16)
    key_rows = projected[1].astype(jnp.bfloat16)
    value_rows = (projected[2] + bias_pair[1]).astype(jnp.bfloat16)
    keys_all, values_all = (
        lax.all_gather(key_rows, "ctx", axis=0, tiled=True),
        lax.all_gather(value_rows, "ctx", axis=0, tiled=True),
    )
    query_heads = queries.reshape(tokens, heads_here, HD).transpose(1, 0, 2)
    width_block = min(512, group_len)
    count_blocks = group_len // width_block
    key_blocks = keys_all.reshape(count_blocks, width_block, heads_here, HD)
    value_blocks = values_all.reshape(count_blocks, width_block, heads_here, HD)
    seg_blocks = seg_all.reshape(count_blocks, width_block)

    def scores_of(key_block, seg_block):
        raw = 0.125 * jnp.einsum(
            "htd,khd->htk", query_heads, key_block, preferred_element_type=jnp.float32
        )
        return jnp.where((seg_query[:, None] == seg_block[None, :])[None], raw, neg_large)

    def running_stats(carry, element):
        top_now, mass = carry
        scores = scores_of(element[0], element[1])
        top_next = jnp.maximum(top_now, jnp.max(scores, -1))
        mass = mass * jnp.exp(top_now - top_next) + jnp.sum(
            jnp.exp(scores - top_next[..., None]), -1
        )
        return ((top_next, mass), None)

    start_top = jnp.full((heads_here, tokens), neg_large, jnp.float32)
    (top_final, mass_final), unused = lax.scan(
        running_stats, (start_top, jnp.zeros_like(start_top)), (key_blocks, seg_blocks)
    )
    log_mass = top_final + jnp.log(mass_final)

    def mix_values(accum, element):
        probs = jnp.exp(scores_of(element[0], element[2]) - log_mass[..., None]).astype(
            jnp.bfloat16
        )
        return (
            accum
            + jnp.einsum("htk,khd->htd", probs, element[1], preferred_element_type=jnp.float32),
            None,
        )

    blocks_all = (key_blocks, value_blocks, seg_blocks)
    attended, unused = lax.scan(
        mix_values, jnp.zeros((heads_here, tokens, HD), jnp.float32), blocks_all
    )
    attended_rows = attended.transpose(1, 0, 2).reshape(tokens, local_width).astype(jnp.bfloat16)
    branch_part = jnp.einsum(
        "te,de->td", attended_rows, out_full, preferred_element_type=jnp.float32
    )
    branch = lax.psum(branch_part.astype(jnp.bfloat16), "tensor").astype(
        jnp.float32
    ) + b_out.astype(jnp.float32)
    first_gain = ln1_gain.astype(jnp.float32)
    second_gain = ln2_gain.astype(jnp.float32)
    hidden, first_normal, first_scale = layer_norm(
        inputs.astype(jnp.float32) + branch, first_gain, ln1_bias.astype(jnp.float32)
    )
    hidden_low = hidden.astype(jnp.bfloat16)
    pre_act = jnp.dot(hidden_low, up_full, preferred_element_type=jnp.float32) + b_up.astype(
        jnp.float32
    )
    activated = gelu_exact(pre_act).astype(jnp.bfloat16)
    second_part = jnp.einsum("tf,df->td", activated, down_full, preferred_element_type=jnp.float32)
    second_branch = lax.psum(second_part.astype(jnp.bfloat16), "tensor").astype(
        jnp.float32
    ) + b_down.astype(jnp.float32)
    result, second_normal, second_scale = layer_norm(
        hidden + second_branch, second_gain, ln2_bias.astype(jnp.float32)
    )
    qkv_full, out_full, up_full, down_full = (
        lax.all_gather(w_qkv, ("shard", "ctx"), axis=0, tiled=True),
        lax.all_gather(w_out, ("shard", "ctx"), axis=0, tiled=True),
        lax.all_gather(w_up, ("shard", "ctx"), axis=0, tiled=True),
        lax.all_gather(w_down, ("shard", "ctx"), axis=0, tiled=True),
    )
    upstream = cotangent[0].astype(jnp.float32)
    second_grad, grad_gain_two, grad_bias_two = norm_back(
        upstream, second_normal, second_scale, second_gain
    )
    grad_down_bias = jnp.sum(second_grad, 0)
    second_low = second_grad.astype(jnp.bfloat16)
    grad_down = jnp.einsum("td,tf->df", second_low, activated, preferred_element_type=jnp.float32)
    act_grad = jnp.einsum("td,df->tf", second_low, down_full, preferred_element_type=jnp.float32)
    pre_grad = act_grad * gelu_slope(pre_act)
    grad_up_bias = jnp.sum(pre_grad, 0)
    pre_low = pre_grad.astype(jnp.bfloat16)
    grad_up = jnp.einsum("td,tf->df", hidden_low, pre_low, preferred_element_type=jnp.float32)
    hidden_part = jnp.einsum("tf,df->td", pre_low, up_full, preferred_element_type=jnp.float32)
    hidden_grad = second_grad + lax.psum(hidden_part.astype(jnp.bfloat16), "tensor").astype(
        jnp.float32
    )
    first_grad, grad_gain_one, grad_bias_one = norm_back(
        hidden_grad, first_normal, first_scale, first_gain
    )
    grad_out_bias = jnp.sum(first_grad, 0)
    first_low = first_grad.astype(jnp.bfloat16)
    grad_out = jnp.einsum("td,te->de", first_low, attended_rows, preferred_element_type=jnp.float32)
    attended_grad = jnp.einsum(
        "td,de->te", first_low, out_full, preferred_element_type=jnp.float32
    ).astype(jnp.bfloat16)
    grad_heads = attended_grad.reshape(tokens, heads_here, HD).transpose(1, 0, 2)
    row_delta = jnp.sum(grad_heads.astype(jnp.float32) * attended, -1)

    def prob_pair(element):
        probs = jnp.exp(scores_of(element[0], element[2]) - log_mass[..., None])
        prob_grad = jnp.einsum(
            "htd,khd->htk", grad_heads, element[1], preferred_element_type=jnp.float32
        )
        return (probs, prob_grad)

    zero_heads = jnp.zeros((heads_here, tokens, HD), jnp.float32)

    def score_grads(accum, element):
        probs, prob_grad = prob_pair(element)
        score_grad = (probs * (prob_grad - row_delta[..., None])).astype(jnp.bfloat16)
        accum = accum + 0.125 * jnp.einsum(
            "htk,khd->htd", score_grad, element[0], preferred_element_type=jnp.float32
        )
        key_grad = 0.125 * jnp.einsum(
            "htk,htd->khd", score_grad, query_heads, preferred_element_type=jnp.float32
        )
        value_grad = jnp.einsum(
            "htk,htd->khd",
            probs.astype(jnp.bfloat16),
            grad_heads,
            preferred_element_type=jnp.float32,
        )
        return (accum, (key_grad, value_grad))

    query_grad, (key_parts, value_parts) = lax.scan(score_grads, zero_heads, blocks_all)
    key_sum, value_sum = (
        lax.psum_scatter(
            key_parts.reshape(group_len, local_width).astype(jnp.bfloat16),
            "ctx",
            scatter_dimension=0,
            tiled=True,
        ).astype(jnp.float32),
        lax.psum_scatter(
            value_parts.reshape(group_len, local_width).astype(jnp.bfloat16),
            "ctx",
            scatter_dimension=0,
            tiled=True,
        ).astype(jnp.float32),
    )
    query_rows = query_grad.transpose(1, 0, 2).reshape(tokens, local_width)
    bias_grads = jnp.stack([jnp.sum(query_rows, 0), jnp.sum(value_sum, 0)])
    stacked = jnp.stack([query_rows, key_sum, value_sum]).astype(jnp.bfloat16)
    grad_qkv = jnp.einsum("td,wte->dwe", inputs, stacked, preferred_element_type=jnp.float32)
    input_part = jnp.einsum("wte,dwe->td", stacked, qkv_full, preferred_element_type=jnp.float32)
    grad_inputs = first_grad + lax.psum(input_part.astype(jnp.bfloat16), "tensor").astype(
        jnp.float32
    )
    matrices = (
        lax.psum_scatter(grad_qkv, ("shard", "ctx"), scatter_dimension=0, tiled=True),
        lax.psum_scatter(grad_out, ("shard", "ctx"), scatter_dimension=0, tiled=True),
        lax.psum_scatter(grad_up, ("shard", "ctx"), scatter_dimension=0, tiled=True),
        lax.psum_scatter(grad_down, ("shard", "ctx"), scatter_dimension=0, tiled=True),
    )
    vectors = lax.psum(
        (
            bias_grads,
            grad_out_bias,
            grad_gain_one,
            grad_bias_one,
            grad_up_bias,
            grad_down_bias,
            grad_gain_two,
            grad_bias_two,
        ),
        ("shard", "ctx"),
    )
    return (
        result.astype(jnp.bfloat16)[None],
        grad_inputs[None],
        matrices[0],
        vectors[0],
        matrices[1],
        vectors[1],
        vectors[2],
        vectors[3],
        matrices[2],
        vectors[4],
        matrices[3],
        vectors[5],
        vectors[6],
        vectors[7],
    )


def solution(mesh):
    return jax.shard_map(
        on_device,
        mesh=mesh,
        in_specs=(
            P("shard", "ctx", None),
            P("shard", None),
            P(("shard", "ctx"), None, "tensor"),
            P(None, "tensor"),
            P(("shard", "ctx"), "tensor"),
            P(),
            P(),
            P(),
            P(("shard", "ctx"), "tensor"),
            P("tensor"),
            P(("shard", "ctx"), "tensor"),
            P(),
            P(),
            P(),
            P("shard", "ctx", None),
        ),
        out_specs=(
            P("shard", "ctx", None),
            P("shard", "ctx", None),
            P(("shard", "ctx"), None, "tensor"),
            P(None, "tensor"),
            P(("shard", "ctx"), "tensor"),
            P(),
            P(),
            P(),
            P(("shard", "ctx"), "tensor"),
            P("tensor"),
            P(("shard", "ctx"), "tensor"),
            P(),
            P(),
            P(),
        ),
        check_vma=False,
    )
```

profile of v0, /device:TPU:0, one launch (start us, length us, event | category | flops | bytes accessed | tf_op | source)
XLA Modules:
  0.0 909.8 jit_solution(9151081868112059575)
XLA Ops:
  8.0 45.4 %all-gather.7.cloned.1.call-done = bf16[768,3,384]{2,0,1:T(8,128)(2,1)} async-done(((bf16[48,3,384]{2,0,1:T(8,128)(2,1)}), bf16[768,3,384]{2,0,1:T(8,128)(2,1)}) %all-gather.7.cloned.1.call-update) | async-done | bytes 1769488 | tf_op jit(solution)/shard_map/all_gather | solution.py:63
  53.4 2.8 convolution_bitcast_fusion.1
  59.9 47.4 %all_gather.25 = bf16[768,384]{1,0:T(8,128)(2,1)} all-gather(bf16[48,384]{1,0:T(8,128)(2,1)S(1)} %copy-done.32), channel_id=1, replica_groups=mesh['shard'=4,'ctx'=4,'tensor'=2] {'shard','ctx'}, dimensions={0}, use_global_device_ids=true | all-gather | bytes 626688 | tf_op jit(solution)/shard_map/all_gather | solution.py:64
  107.3 2.0 fusion.72
  109.5 3.9 reshape.191
  113.3 1.8 copy.64
  115.2 33.0 %while.39 = (s32[]{:T(128)}, f32[6,512]{1,0:T(8,128)S(1)}, f32[6,512]{1,0:T(8,128)S(1)}, s32[512]{0:T(512)S(1)}, s32[4,512]{1,0:T(4,128)S(1)}, /*index=5*/bf16[4...) while((s32[]{:T(128)}, f32[6,512]{1,0:T(8,128)S(1)}, ...), condition=%wide.region_3.4_spmd.clone, body=%wide.region_0.3_spmd.clone.sunk | while | flops 212614144 | bytes 14323824 | solution.py:102
  115.4 3.9 fusion.139
  119.3 4.1 exponential_reduce_fusion.2
  123.7 3.9 fusion.139
  127.6 4.1 exponential_reduce_fusion.2
  132.0 3.9 fusion.139
  135.8 4.1 exponential_reduce_fusion.2
  140.2 3.9 fusion.139
  144.1 4.1 exponential_reduce_fusion.2
  148.3 3.9 reshape.192
  152.1 2.9 copy.65
  155.0 14.4 %while.40 = (s32[]{:T(128)}, f32[6,512,64]{1,2,0:T(8,128)S(1)}, s32[512]{0:T(512)S(1)}, s32[4,512]{1,0:T(4,128)S(1)}, bf16[4,512,6,64]{1,3,2,0:T(8,128)(2,1)S(1)...) while((s32[]{:T(128)}, f32[6,512,64]{1,2,0:T(8,128)S(1)}, ...), condition=%wide.region_5.6_spmd.clone, body=%wide.region_4.5_spmd.clone.sunk | while | flops 409600000 | bytes 3302515 | solution.py:118
  155.3 3.3 fusion.145
  158.9 3.3 fusion.145
  162.5 3.3 fusion.145
  166.1 3.3 fusion.145
  171.2 2.6 convolution_convert_fusion.2
  175.2 30.2 %all-reduce.8.cloned.1.call-done = bf16[512,768]{1,0:T(8,128)(2,1)} async-done(((bf16[512,768]{1,0:T(8,128)(2,1)}), bf16[512,768]{1,0:T(8,128)(2,1)}) %all-reduce.8.cloned.1.call-update) | async-done | bytes 786448 | tf_op jit(solution)/shard_map/psum | solution.py:125
  207.5 42.7 %all-gather.11.cloned.1.call-done = bf16[768,1536]{1,0:T(8,128)(2,1)} async-done(((bf16[48,1536]{1,0:T(8,128)(2,1)}), bf16[768,1536]{1,0:T(8,128)(2,1)}) %all-gather.11.cloned.1.call-update) | async-done | bytes 2359312 | tf_op jit(solution)/shard_map/all_gather | solution.py:65
  250.2 5.8 multiply_convert_fusion
  255.9 37.7 %all-gather.13.cloned.1.call-done = bf16[768,1536]{1,0:T(8,128)(2,1)} async-done(((bf16[48,1536]{1,0:T(8,128)(2,1)}), bf16[768,1536]{1,0:T(8,128)(2,1)}) %all-gather.13.cloned.1.call-update) | async-done | bytes 2359312 | tf_op jit(solution)/shard_map/all_gather | solution.py:66
  293.7 4.5 convolution_convert_fusion.1
  298.3 33.1 %all-reduce.10.cloned.1.call-done = bf16[512,768]{1,0:T(8,128)(2,1)} async-done(((bf16[512,768]{1,0:T(8,128)(2,1)}), bf16[512,768]{1,0:T(8,128)(2,1)}) %all-reduce.10.cloned.1.call-update) | async-done | bytes 786448 | tf_op jit(solution)/shard_map/psum | solution.py:139
  331.4 2.1 fusion.91
  337.8 3.1 fusion.92
  342.1 2.3 convolution_convert_fusion
  344.7 34.2 %all-reduce.12.cloned.1.call-done = bf16[512,768]{1,0:T(8,128)(2,1)} async-done(((bf16[512,768]{1,0:T(8,128)(2,1)}), bf16[512,768]{1,0:T(8,128)(2,1)}) %all-reduce.12.cloned.1.call-update) | async-done | bytes 786448 | tf_op jit(solution)/shard_map/psum | solution.py:164
  378.9 3.6 multiply_reduce_fusion
  386.3 60.3 %while.41 = (s32[]{:T(128)}, f32[6,512,64]{1,2,0:T(8,128)}, bf16[4,512,6,64]{1,3,2,0:T(8,128)(2,1)}, bf16[4,512,6,64]{1,3,2,0:T(8,128)(2,1)}, s32[512]{0:T(512)S...) while((s32[]{:T(128)}, f32[6,512,64]{1,2,0:T(8,128)}, ...), condition=%wide.region_19.20_spmd.clone, body=%wide.region_18.19_spmd.clone.sunk | while | flops 1023410176 | bytes 78191024 | solution.py:205
  387.8 3.6 fusion.157
  391.4 1.8 fusion.159
  393.2 2.7 fusion.158
  395.9 5.3 fusion.160
  402.7 3.6 fusion.157
  406.2 1.8 fusion.159
  408.1 2.9 fusion.158
  411.0 5.3 fusion.160
  417.8 3.6 fusion.157
  423.2 2.9 fusion.158
  426.2 5.3 fusion.160
  432.9 3.6 fusion.157
  438.4 2.9 fusion.158
  441.3 5.3 fusion.160
  446.6 2.6 copy.70
  451.6 2.6 copy.68
  457.7 29.1 %reduce-scatter.8.cloned.1.call-done = bf16[512,384]{1,0:T(8,128)(2,1)} async-done(((bf16[2048,384]{1,0:T(8,128)(2,1)}), bf16[512,384]{1,0:T(8,128)(2,1)}) %reduce-scatter.8.cloned.1.call-update) | async-done | bytes 393232 | tf_op jit(solution)/shard_map/reduce_scatter | solution.py:213
  486.8 36.5 %reduce-scatter.6.cloned.1.call-done = bf16[512,384]{1,0:T(8,128)(2,1)} async-done(((bf16[2048,384]{1,0:T(8,128)(2,1)}), bf16[512,384]{1,0:T(8,128)(2,1)}) %reduce-scatter.6.cloned.1.call-update) | async-done | bytes 393232 | tf_op jit(solution)/shard_map/reduce_scatter | solution.py:207
  523.3 4.0 bitcast_convert_fusion
  527.4 2.9 convolution_bitcast_fusion
  530.3 6.3 copy.74
  539.8 5.5 fusion.75
  545.4 5.4 fusion.82
  554.0 63.4 %all-reduce.1 = (f32[2,384]{1,0:T(2,128)}, f32[768]{0:T(1024)}, f32[768]{0:T(1024)}, f32[768]{0:T(1024)}, f32[1536]{0:T(1024)}, /*index=5*/f32[768]{0:T(1024)}, f32[768]{0:T(1024)}, f32[768]{0:T(1024)}) all-reduce(f32[2,384]{1,0:T(2,128)S(1)} %pad_maximum_fusion.3, ...), channel_id=1, replica_groups=mesh['shard'=4,'ctx'=4,'tensor'=2] {'shard','ctx'}, use_global_device_ids=true, to_apply=%region_26.27 | all-reduce | flops 6912 | bytes 55296 | tf_op jit(solution)/shard_map/psum | solution.py:234
  617.4 2.4 add_bitcast_fusion
  619.9 62.7 %all-reduce.16.cloned.1.call-done = f32[768,3,384]{2,1,0:T(4,128)} async-done(((f32[768,3,384]{2,1,0:T(4,128)}), f32[768,3,384]{2,1,0:T(4,128)}) %all-reduce.16.cloned.1.call-update) | async-done | bytes 3538960
  684.3 60.2 %reduce-scatter.10.cloned.1.call-done = f32[48,384]{1,0:T(8,128)} async-done(((f32[768,384]{1,0:T(8,128)}), f32[48,384]{1,0:T(8,128)}) %reduce-scatter.10.cloned.1.call-update) | async-done | bytes 73744 | tf_op jit(solution)/shard_map/reduce_scatter | solution.py:230
  744.5 78.9 %reduce-scatter.12.cloned.1.call-done = f32[48,1536]{1,0:T(8,128)} async-done(((f32[768,1536]{1,0:T(8,128)}), f32[48,1536]{1,0:T(8,128)}) %reduce-scatter.12.cloned.1.call-update) | async-done | bytes 294928 | tf_op jit(solution)/shard_map/reduce_scatter | solution.py:231
  823.4 79.4 %reduce-scatter.14.cloned.1.call-done = f32[48,1536]{1,0:T(8,128)} async-done(((f32[768,1536]{1,0:T(8,128)}), f32[48,1536]{1,0:T(8,128)}) %reduce-scatter.14.cloned.1.call-update) | async-done | bytes 294928 | tf_op jit(solution)/shard_map/reduce_scatter | solution.py:232
  (306 shorter events, 43.4 us)
Async XLA Ops:
  7.2 46.2 %all-gather.7.cloned.1.call-start = ((), (), s32[]{:S(2)}) async-start(), calls=%async_computation.5 | async-start | bytes 1880064 | tf_op jit(solution)/shard_map/all_gather | solution.py:63
  7.9 50.6 %copy-start.51 = (bf16[2,384]{1,0:T(2,128)(2,1)S(1)}, bf16[2,384]{1,0:T(2,128)(2,1)}, u32[]{:S(2)}) copy-start(bf16[2,384]{1,0:T(2,128)(2,1)} %param.24) | copy-start | bytes 4612
  7.9 51.2 %copy-start.43 = (s32[1,2048]{1,0:T(1,128)S(1)}, s32[1,2048]{1,0:T(1,128)}, u32[]{:S(2)}) copy-start(s32[1,2048]{1,0:T(1,128)} %param.22) | copy-start | bytes 24580
  7.9 51.9 %copy-start.32 = (bf16[48,384]{1,0:T(8,128)(2,1)S(1)}, bf16[48,384]{1,0:T(8,128)(2,1)}, u32[]{:S(2)}) copy-start(bf16[48,384]{1,0:T(8,128)(2,1)} %param.25) | copy-start | bytes 110596
  7.9 101.5 %all-gather.15.cloned.1.call-start = ((), (), s32[]{:S(2)}) async-start(), calls=%async_computation.18 | async-start | bytes 1966080 | tf_op jit(solution)/shard_map/all_gather | solution.py:76
  58.4 89.8 %all-gather.9.cloned.1.call-start = ((), (), s32[]{:S(2)}) async-start(), calls=%async_computation.6 | async-start | bytes 1966080 | tf_op jit(solution)/shard_map/all_gather | solution.py:77
  59.9 49.4 %slice-start = ((f32[3,512,384]{1,2,0:T(8,128)}), f32[1,512,384]{1,2,0:T(8,128)S(1)}, s32[]{:S(2)}) async-start(f32[3,512,384]{1,2,0:T(8,128)} %copy-done.22), calls=%async_computation.20 | async-start | bytes 1572864 | tf_op jit(solution)/shard_map/slice | solution.py:72
  109.4 96.0 %all-reduce.8.cloned.1.call-start = ((), (), s32[]{:S(2)}) async-start(), calls=%async_computation.7 | async-start | bytes 1572864 | tf_op jit(solution)/shard_map/psum | solution.py:125
  170.4 4.7 copy-start.45
  170.4 4.7 copy-start.46
  170.4 4.7 copy-start.47
  170.4 4.8 copy-start.44
  170.4 35.0 %copy-start.8 = (bf16[1,512,768]{2,1,0:T(8,128)(2,1)S(1)}, bf16[1,512,768]{2,1,0:T(8,128)(2,1)}, u32[]{:S(2)}) copy-start(bf16[1,512,768]{2,1,0:T(8,128)(2,1)} %param.21) | copy-start | bytes 2359300
  173.7 76.4 %all-gather.11.cloned.1.call-start = ((), (), s32[]{:S(2)}) async-start(), calls=%async_computation.8 | async-start | bytes 2506752 | tf_op jit(solution)/shard_map/all_gather | solution.py:65
  174.3 119.3 %all-gather.13.cloned.1.call-start = ((), (), s32[]{:S(2)}) async-start(), calls=%async_computation.9 | async-start | bytes 2506752 | tf_op jit(solution)/shard_map/all_gather | solution.py:66
  174.9 156.5 %all-reduce.10.cloned.1.call-start = ((), (), s32[]{:S(2)}) async-start(), calls=%async_computation.10 | async-start | bytes 1572864 | tf_op jit(solution)/shard_map/psum | solution.py:139
  175.2 207.3 %copy-start.28 = (f32[768]{0:T(1024)}, f32[768]{0:T(1024)S(1)}, u32[]{:S(2)}) copy-start(f32[768]{0:T(1024)S(1)} %convert_element_type.138) | copy-start | bytes 9220
  175.2 156.2 %copy-start.42 = (f32[768]{0:T(1024)}, f32[768]{0:T(1024)S(1)}, u32[]{:S(2)}) copy-start(f32[768]{0:T(1024)S(1)} %convert_element_type.139) | copy-start | bytes 9220
  207.0 175.5 %copy-start.30 = (f32[512]{0:T(512)}, f32[512]{0:T(512)S(1)}, u32[]{:S(2)}) copy-start(f32[512]{0:T(512)S(1)} %broadcast_multiply_fusion.5) | copy-start | bytes 6148
  207.5 175.0 %copy-start.33 = (f32[512]{0:T(512)}, f32[512]{0:T(512)S(1)}, u32[]{:S(2)}) copy-start(f32[512]{0:T(512)S(1)} %add_rsqrt_fusion.1) | copy-start | bytes 6148
  293.6 4.6 copy-start.48
  293.6 4.6 copy-start.49
  293.7 4.6 copy-start.50
  298.2 80.7 %all-reduce.12.cloned.1.call-start = ((), (), s32[]{:S(2)}) async-start(), calls=%async_computation.11 | async-start | bytes 1572864 | tf_op jit(solution)/shard_map/psum | solution.py:164
  334.6 3.1 copy-start.56
  337.7 3.2 copy-start.6
  337.8 4.3 copy-start.52
  344.4 142.4 %reduce-scatter.8.cloned.1.call-start = ((), (), s32[]{:S(2)}) async-start(), calls=%async_computation.13 | async-start | bytes 1966080 | tf_op jit(solution)/shard_map/reduce_scatter | solution.py:213
  378.9 3.6 copy-start.7
  378.9 3.6 copy-start.11
  378.9 3.7 copy-start.21
  387.5 3.8 copy-start
  387.7 3.6 copy-start.14
  395.9 5.3 copy-start.3
  395.9 5.3 copy-start.41
  402.4 3.8 copy-start
  402.6 3.6 copy-start.14
  411.0 5.4 copy-start.3
  411.0 5.4 copy-start.41
  417.6 3.8 copy-start
  417.8 3.6 copy-start.14
  426.1 5.4 copy-start.3
  426.1 5.3 copy-start.41
  432.7 3.8 copy-start
  432.9 3.6 copy-start.14
  441.3 5.4 copy-start.3
  441.3 5.4 copy-start.41
  451.3 72.0 %reduce-scatter.6.cloned.1.call-start = ((), (), s32[]{:S(2)}) async-start(), calls=%async_computation.12 | async-start | bytes 1966080 | tf_op jit(solution)/shard_map/reduce_scatter | solution.py:207
  456.3 161.2 %all-reduce.14.cloned.1.call-start = ((), (), s32[]{:S(2)}) async-start(), calls=%async_computation.14 | async-start | bytes 1572864 | tf_op jit(solution)/shard_map/psum | solution.py:225
  523.3 4.0 copy-start.9
  523.3 4.0 copy-start.26
  523.3 4.1 copy-start.54
  527.3 155.3 %all-reduce.16.cloned.1.call-start = ((), (), s32[]{:S(2)}) async-start(), calls=%async_computation.19 | async-start | bytes 9437184
  536.6 3.2 copy-start.29
  536.6 3.2 copy-start.31
  536.6 3.2 copy-start.34
  536.6 207.9 %reduce-scatter.10.cloned.1.call-start = ((), (), s32[]{:S(2)}) async-start(), calls=%async_computation.15 | async-start | bytes 1253376 | tf_op jit(solution)/shard_map/reduce_scatter | solution.py:230
  539.7 283.7 %reduce-scatter.12.cloned.1.call-start = ((), (), s32[]{:S(2)}) async-start(), calls=%async_computation.16 | async-start | bytes 5013504 | tf_op jit(solution)/shard_map/reduce_scatter | solution.py:231
  545.4 357.4 %reduce-scatter.14.cloned.1.call-start = ((), (), s32[]{:S(2)}) async-start(), calls=%async_computation.17 | async-start | bytes 5013504 | tf_op jit(solution)/shard_map/reduce_scatter | solution.py:232
  550.9 3.0 copy-start.27
  550.9 3.1 copy-start.36
  550.9 3.1 copy-start.37
  550.9 3.1 copy-start.38
  550.9 3.1 copy-start.39
  (39 other events, 65.9 us)
Sparse Core Ops, SparseCore 0:
  10.3 43.0 all-gather.6
  58.5 44.3 all-gather.14
  109.5 34.3 all-gather.8
  173.8 31.5 all-reduce.7
  207.9 42.2 all-gather.10
  252.6 41.0 all-gather.12
  298.3 33.0 all-reduce.9
  344.5 34.3 all-reduce.11
  451.4 35.2 reduce-scatter.7
  489.0 34.2 reduce-scatter.5
  527.4 33.2 all-reduce.13
  564.2 118.3 all-reduce.15
  686.8 57.6 reduce-scatter.9
  748.8 74.5 reduce-scatter.11
  828.2 74.5 reduce-scatter.13
where the time goes:
time: 918 us; the launch traced here: 910 us
  waiting for transfers between devices  572 us (62%)
  matrix products  128 us (14%)
  blocking collectives  111 us (12%)
  local copies, waits for them, and re-layouts  42.3 us (5%)
  other arithmetic  38.6 us (4%)
  between operations  15.8 us (2%)
    reduce_scatter x1, waiting for transfers between devices, on_device(): lax.psum_scatter(grad_down, ('shard', 'ctx'), scatter_dimension=0, tiled=...  79.4 us
    reduce_scatter x1, waiting for transfers between devices, on_device(): lax.psum_scatter(grad_up, ('shard', 'ctx'), scatter_dimension=0, tiled=True)  78.9 us
    unnamed x16, waiting for transfers between devices  64.7 us
    psum x1, blocking collectives, on_device(): lax.psum((bias_grads, grad_out_bias, grad_gain_one, grad_bias_one, grad_u...  63.4 us
    reduce_scatter x1, waiting for transfers between devices, on_device(): lax.psum_scatter(grad_out, ('shard', 'ctx'), scatter_dimension=0, tiled=T...  60.2 us
    all_gather x1, blocking collectives, on_device(): lax.all_gather(w_out, ('shard', 'ctx'), axis=0, tiled=True)  47.4 us
    all_gather x1, waiting for transfers between devices, on_device(): lax.all_gather(w_qkv, ('shard', 'ctx'), axis=0, tiled=True)  45.4 us
    all_gather x1, waiting for transfers between devices, on_device(): lax.all_gather(w_up, ('shard', 'ctx'), axis=0, tiled=True)  42.7 us
  transfers between devices with their start and end apart: 15, of which 12 were waited for; matrix products, arithmetic and copies ran while one was open for 9% of the time, Pallas kernels for 0%

commit v1 on v0

--- a/solution.py
+++ b/solution.py
@@ -1,22 +1,673 @@
+import math
+
 import jax
 import jax.numpy as jnp
 from jax import lax
+from jax.experimental import pallas as pl
+from jax.experimental.pallas import tpu as pltpu
+from jax.sharding import Mesh
 from jax.sharding import PartitionSpec as P
 
 HD = 64
+LANES = 128
+BF = jnp.bfloat16
+F32 = jnp.float32
+NT = (((1,), (1,)), ((), ()))
+NN = (((1,), (0,)), ((), ()))
+EVERY = ("y", "core", "ctx", "tensor")
+SWAP = ((0, 1), (1, 0))
+
+
+def mm(a, b, dims=NN):
+    return lax.dot_general(a, b, dims, preferred_element_type=F32)
+
+
+def params(mib):
+    return pltpu.CompilerParams(vmem_limit_bytes=mib << 20)
+
+
+def anywhere():
+    return pl.BlockSpec(memory_space=pl.ANY)
+
+
+def whole(shape):
+    return pl.BlockSpec(shape, lambda *_: (0,) * len(shape))
+
+
+def scalars():
+    return pl.BlockSpec(memory_space=pltpu.SMEM)
+
+
+def owner_of(ids, piece, ctx):
+    rc, ry, rx, rz = piece
+    y = (ids[0] + ry) % 2
+    core = (ids[1] + rc) % 2
+    place = (ids[2] + (ctx - rz)) % ctx
+    return (y * 2 + core) * ctx + place, (ids[3] + rx) % 2
+
+
+def piece_copies(ids, refs, layout, full, sem, ctx, rows, width, back=False, base=0):
+    copies = []
+    for ref, pieces, at in zip(refs, layout, range(len(refs))):
+        for index, piece in pieces:
+            block, half = owner_of(ids, piece, ctx)
+            row = pl.multiple_of(block * rows, 16)
+            column = pl.multiple_of(half * width, LANES)
+            if len(full.shape) == 3:
+                there = full.at[:, pl.ds(row, rows), pl.ds(column, width)]
+            else:
+                there = full.at[pl.ds(row, rows), pl.ds(column, width)]
+            here = ref.at[index]
+            source, target = (there, here) if back else (here, there)
+            copies.append(pltpu.make_async_copy(source, target, sem.at[base + len(copies)]))
+    return copies
+
+
+def prepare_kernel(ctx, rows, width, layout, n, heads, scale, ids, xt, bq, *rest):
+    pieces, (weights, queries, sem) = rest[:n], rest[n:]
+    copies = piece_copies(ids, pieces, layout, weights, sem, ctx, rows, width)
+    for copy in copies:
+        copy.start()
+    for copy in copies:
+        copy.wait()
+    tokens = xt.shape[0]
+    lane = lax.broadcasted_iota(jnp.int32, (tokens, LANES), 1)
+    projected = mm(xt[...], weights[0]) + bq[...]
+    projected = (projected.astype(BF).astype(F32) * scale)
+    for pair in range(heads // 2):
+        two = projected[:, pair * LANES : (pair + 1) * LANES]
+        even = jnp.where(lane < HD, two, 0.0).astype(BF)
+        odd = jnp.where(lane >= HD, two, 0.0).astype(BF)
+        queries[pair] = jnp.concatenate([even, odd], 0)
+
+
+def attend_kernel(first, xa, xb, wk, wv, bv, queries, qmark, kmark, *rest):
+    if first:
+        keys, values, keys_t, top_out, sums_out = rest
+    else:
+        top_in, sums_in, keys, values, keys_t, top_out, sums_out = rest
+    x = jnp.concatenate([xa[...], xb[...]], 0)
+    k4 = mm(x, wk[...]).astype(BF)
+    v4 = mm(x, wv[...]) + bv[...]
+    keys[...] = k4
+    values[...] = v4.astype(BF)
+    keys_t[...] = k4.T
+    v4t = v4.T.astype(BF)
+    ones = jnp.ones((16, x.shape[0]), BF)
+    for j in range(2):
+        span = slice(j * LANES, (j + 1) * LANES)
+        kk = jnp.concatenate([k4[:, span], kmark[...]], 1)
+        qq = jnp.concatenate([queries[j], qmark[...]], 1)
+        scores = mm(kk, qq, NT)
+        top = jnp.max(scores, 0, keepdims=True)
+        if not first:
+            top = jnp.maximum(top, top_in[j])
+        probs = jnp.exp(scores - top).astype(BF)
+        sums = mm(jnp.concatenate([v4t[span], ones], 0), probs)
+        if not first:
+            sums = sums + sums_in[j] * jnp.exp(top_in[j] - top)
+        top_out[j] = top
+        sums_out[j] = sums
+
+
+def normed(z, eps=1e-05):
+    centred = z - jnp.mean(z, -1, keepdims=True)
+    factor = lax.rsqrt(jnp.mean(centred * centred, -1, keepdims=True) + eps)
+    return centred * factor, factor
+
+
+def norm_back(e, n, factor, gain):
+    scaled = e * gain
+    return factor * (
+        scaled - jnp.mean(scaled, -1, keepdims=True) - n * jnp.mean(scaled * n, -1, keepdims=True)
+    )
+
+
+def total(v):
+    return jnp.sum(v, 0, keepdims=True)
+
+
+def middle_kernel(ctx, rows, lay_up, lay_down, lay_out, n_up, n_down, heads, ids, sums, top, xt, cot, vec, b_up, *rest):
+    ups, rest = rest[:n_up], rest[n_up:]
+    downs, rest = rest[:n_down], rest[n_down:]
+    (
+        out_ref, dz1_ref, dos, lse, delta, vgrads, gup_bias,
+        u_ref, dpb_ref, h1b_ref, dmb_ref, dzb_ref, ob_ref,
+        wup, wdown, wout, pre_s, prod, sem_up, sem_down, sem_out,
+    ) = rest
+    width = wup.shape[1] // 2
+    owidth = wout.shape[1] // 2
+    out_part = [d.at[..., width : width + owidth] for d in downs]
+    down_part = [d.at[..., 0:width] for d in downs]
+    c_out = piece_copies(ids, out_part, lay_out, wout, sem_out, ctx, rows, owidth)
+    c_up = piece_copies(ids, ups, lay_up, wup, sem_up, ctx, rows, width)
+    c_down = piece_copies(ids, down_part, lay_down, wdown, sem_down, ctx, rows, width)
+    for copy in c_out + c_up + c_down:
+        copy.start()
+    tokens, model = xt.shape
+    pairs = heads // 2
+    half = tokens
+    parts = []
+    for p in range(pairs):
+        mass = sums[p, LANES : LANES + 1, :]
+        ot = sums[p, 0:LANES, :] / mass
+        lse[p] = top[p] + jnp.log(mass)
+        parts.append(jnp.concatenate([ot[0:HD, 0:half], ot[HD:LANES, half : 2 * half]], 0).T)
+    o = jnp.concatenate(parts, 1)
+    ob = o.astype(BF)
+    ob_ref[...] = ob
+    for copy in c_out:
+        copy.wait()
+    b_out, g1, b1, b_down, g2, b2 = (vec[i : i + 1, :] for i in range(6))
+    z1 = xt[...].astype(F32) + mm(ob, wout[...], NT) + b_out
+    n1, f1 = normed(z1)
+    h1 = n1 * g1 + b1
+    h1b = h1.astype(BF)
+    h1b_ref[...] = h1b
+    for copy in c_up:
+        copy.wait()
+    hidden = wup.shape[1]
+    step = model
+    for c in range(0, hidden, step):
+        pre = mm(h1b, wup[:, c : c + step]) + b_up[:, c : c + step]
+        pre_s[:, c : c + step] = pre
+        u_ref[:, c : c + step] = (0.5 * pre * (1.0 + lax.erf(pre * 0.7071067811865476))).astype(BF)
+    for copy in c_down:
+        copy.wait()
+    m = mm(u_ref[...], wdown[...], NT) + b_down
+    n2, f2 = normed(h1 + m)
+    out_ref[...] = (n2 * g2 + b2).astype(BF)
+    g = cot[...].astype(F32)
+    dz2 = norm_back(g, n2, f2, g2)
+    dmb = dz2.astype(BF)
+    dmb_ref[...] = dmb
+    vgrads[3:4, :] = total(dz2)
+    vgrads[4:5, :] = total(g * n2)
+    vgrads[5:6, :] = total(g)
+    for c in range(0, hidden, step):
+        pre = pre_s[:, c : c + step]
+        slope = 0.5 * (1.0 + lax.erf(pre * 0.7071067811865476)) + pre * jnp.exp(
+            -0.5 * pre * pre
+        ) * 0.3989422804014327
+        dpre = mm(dmb, wdown[:, c : c + step]) * slope
+        gup_bias[:, c : c + step] = total(dpre)
+        dpb_ref[:, c : c + step] = dpre.astype(BF)
+    dh1 = dz2 + mm(dpb_ref[...], wup[...], NT)
+    dz1 = norm_back(dh1, n1, f1, g1)
+    dz1_ref[...] = dz1
+    vgrads[0:1, :] = total(dz1)
+    vgrads[1:2, :] = total(dh1 * n1)
+    vgrads[2:3, :] = total(dh1)
+    vgrads[6:8, :] = jnp.zeros((2, model), F32)
+    dzb = dz1.astype(BF)
+    dzb_ref[...] = dzb
+    do = mm(dzb, wout[...]).astype(BF).astype(F32)
+    prod[...] = do * o
+    spread = (
+        lax.broadcasted_iota(jnp.int32, (16, model), 1) // HD
+        == lax.broadcasted_iota(jnp.int32, (16, model), 0)
+    ).astype(F32)
+    by_head = lax.dot_general(
+        spread, prod[...], NT, precision=lax.Precision.HIGHEST, preferred_element_type=F32
+    )
+    lane = lax.broadcasted_iota(jnp.int32, (tokens, LANES), 1)
+    for p in range(pairs):
+        two = do[:, p * LANES : (p + 1) * LANES]
+        dos[p] = jnp.concatenate(
+            [jnp.where(lane < HD, two, 0.0).astype(BF), jnp.where(lane >= HD, two, 0.0).astype(BF)], 0
+        )
+        delta[p] = jnp.concatenate([by_head[2 * p : 2 * p + 1], by_head[2 * p + 1 : 2 * p + 2]], 1)
+
+
+def feed_grads_kernel(ctx, rows, lay_up, lay_down, lay_out, ids, h1b, dmb, dzb, ob, u, dpb,
+                      up0, up1, down0, down1, gup, gdown, gout, h1t, dmt, sem_up, sem_down, sem_out):
+    step = pl.program_id(0)
+    model = gup.shape[0]
+    width, owidth = gup.shape[1] // 2, gout.shape[1] // 2
+
+    @pl.when(step == 0)
+    def _():
+        h1t[...] = h1b[...].T
+        dmt[...] = dmb[...].T
+        gout[...] = mm(dzb[...].T, ob[...]).astype(BF)
+
+    span = pl.ds(pl.multiple_of(step * model, LANES), model)
+    gup[:, span] = mm(h1t[...], dpb[...]).astype(BF)
+    gdown[:, span] = mm(dmt[...], u[...]).astype(BF)
+
+    @pl.when(step == pl.num_programs(0) - 1)
+    def _():
+        downs = [down0, down1]
+        copies = piece_copies(ids, [up0, up1], lay_up, gup, sem_up, ctx, rows, width, True)
+        copies += piece_copies(
+            ids, [d.at[..., 0:width] for d in downs], lay_down, gdown, sem_down, ctx, rows, width, True)
+        copies += piece_copies(
+            ids, [d.at[..., width : width + owidth] for d in downs], lay_out, gout, sem_out, ctx, rows, owidth, True)
+        for copy in copies:
+            copy.start()
+        for copy in copies:
+            copy.wait()
+
+
+def attend_back_kernel(first, keys, values, keys_t, queries, qmark, kmark, dos, lse, delta, wk, wv, *rest):
+    if first:
+        dk_ref, dv_ref, dqt_out, gbv, dxa, dxb, dx = rest
+    else:
+        dqt_in, dk_ref, dv_ref, dqt_out, gbv, dxa, dxb, dx = rest
+    step = pl.program_id(0)
+    k4, v4 = keys[...], values[...]
+    dks, dvs = [], []
+    for j in range(2):
+        span = slice(j * LANES, (j + 1) * LANES)
+        kk = jnp.concatenate([k4[:, span], kmark[...]], 1)
+        qq = jnp.concatenate([queries[j], qmark[...]], 1)
+        probs = jnp.exp(mm(kk, qq, NT) - lse[j])
+        ds = (probs * (mm(v4[:, span], dos[j], NT) - delta[j])).astype(BF)
+        dvs.append(mm(probs.astype(BF), dos[j]))
+        dks.append(mm(ds, queries[j]))
+        dqt = mm(keys_t[span], ds)
+        dqt_out[j] = dqt if first else dqt_in[j] + dqt
+    dv4 = jnp.concatenate(dvs, 1)
+    gbv[...] = total(dv4)
+    dkb, dvb = jnp.concatenate(dks, 1).astype(BF), dv4.astype(BF)
+    dk_ref[...] = dkb
+    dv_ref[...] = dvb
+    part = mm(dkb, wk[...], NT) + mm(dvb, wv[...], NT)
+
+    @pl.when(step == 0)
+    def _():
+        dx[...] = part
+
+    @pl.when(step > 0)
+    def _():
+        dx[...] += part
+
+    @pl.when(step == pl.num_programs(0) - 1)
+    def _():
+        half = dxa.shape[0]
+        dxa[...] = dx[0:half].astype(BF)
+        dxb[...] = dx[half:].astype(BF)
+
+
+def last_kernel(ctx, rows, layout, scale, ids, dqt, wq, *rest):
+    blocks = 2 * ctx
+    xs, rest = rest[:blocks], rest[blocks:]
+    dks, rest = rest[:ctx], rest[ctx:]
+    dvs, rest = rest[:ctx], rest[ctx:]
+    dxq, gbq, out0, out1, grads, xts, dx, sem = rest
+    step = pl.program_id(0)
+    half = xs[0].shape[0]
+
+    @pl.when(step == 0)
+    def _():
+        for i in range(blocks):
+            xts[i] = xs[i][...].T
+
+    cols = []
+    for j in range(2):
+        t = dqt[j]
+        cols.append(jnp.concatenate([t[0:HD, 0:half], t[HD:LANES, half : 2 * half]], 0).T)
+    dq = jnp.concatenate(cols, 1) * scale
+    gbq[...] = total(dq)
+    dqb = dq.astype(BF)
+    width = dqb.shape[1]
+    span = pl.ds(pl.multiple_of(step * width, LANES), width)
+    part = mm(dqb, wq[...], NT)
+
+    @pl.when(step == 0)
+    def _():
+        dx[...] = part
+
+    @pl.when(step > 0)
+    def _():
+        dx[...] += part
+
+    grads[0, :, span] = mm(xts[0], dqb).astype(BF)
+    for kind, parts in ((1, dks), (2, dvs)):
+        acc = None
+        for r in range(ctx):
+            for side in range(2):
+                one = mm(xts[2 * r + side], parts[r][side * half : (side + 1) * half, :])
+                acc = one if acc is None else acc + one
+        grads[kind, :, span] = acc.astype(BF)
+
+    @pl.when(step == pl.num_programs(0) - 1)
+    def _():
+        dxq[...] = dx[...]
+        copies = piece_copies(ids, [out0, out1], layout, grads, sem, ctx, rows, grads.shape[2] // 2, True)
+        for copy in copies:
+            copy.start()
+        for copy in copies:
+            copy.wait()
+
+
+def shift(v, by, ctx):
+    return lax.ppermute(v, "ctx", [(i, (i + by) % ctx) for i in range(ctx)])
+
+
+def swap(v, axis):
+    return lax.ppermute(v, axis, SWAP)
+
+
+def gather_pieces(local, ctx, order, axis):
+    rows = local.shape[axis]
+    line = jnp.concatenate([local] + [shift(local, r, ctx) for r in range(1, ctx)], axis)
+    both = jnp.concatenate([line, swap(line, order[0])], axis)
+    far = swap(both, order[1])
+    arrays, layout = [], []
+    for rc in range(2):
+        for second, v in ((0, both), (1, far)):
+            arrays.append(v if rc == 0 else swap(v, "core"))
+            pieces = []
+            for first in range(2):
+                for rz in range(ctx):
+                    at = (first * ctx + rz) * rows
+                    index = (slice(None),) * axis + (slice(at, at + rows),)
+                    rel = {order[0]: first, order[1]: second}
+                    pieces.append((index, (rc, rel["y"], rel["tensor"], rz)))
+            layout.append(pieces)
+    return arrays, layout
+
+
+def scatter_layout(ctx, rows, order, lead):
+    layout = []
+    for rc in range(2):
+        pieces = []
+        for first in range(2):
+            for second in range(2):
+                for rz in range(ctx):
+                    rel = {order[0]: first, order[1]: second}
+                    index = (first, second) + (slice(None),) * lead + (slice(rz * rows, (rz + 1) * rows),)
+                    pieces.append((index, (rc, rel["y"], rel["tensor"], rz)))
+        layout.append(pieces)
+    return layout
+
+
+def add(a, b):
+    return a.astype(F32) + b.astype(F32)
+
+
+def scatter_sum(kept, sent, ctx, rows, order, axis):
+    summed = add(kept, swap(sent, "core"))
+    summed = add(summed[0], swap(summed[1].astype(BF), order[0]))
+    summed = add(summed[0], swap(summed[1].astype(BF), order[1]))
+    pick = lambda r: lax.slice_in_dim(summed, r * rows, (r + 1) * rows, axis=axis)
+    result = pick(0)
+    for r in range(1, ctx):
+        result = result + shift(pick(r).astype(BF), -r, ctx).astype(F32)
+    return result
+
+
+def sum_everywhere(v, ctx):
+    for axis in ("core", "tensor", "y"):
+        v = v + swap(v, axis)
+    bit = 1
+    while bit < ctx:
+        v = v + lax.ppermute(v, "ctx", [(i, i ^ bit) for i in range(ctx)])
+        bit *= 2
+    return v
+
+
+def on_device(
+    layer_input, segments, w_qkv, b_qv, w_out, b_out, ln1_gain, ln1_bias,
+    w_up, b_up, w_down, b_down, ln2_gain, ln2_bias, cotangent,
+):
+    ctx = lax.axis_size("ctx")
+    y, core, z, t = (lax.axis_index(a) for a in EVERY)
+    ids = jnp.stack([y, core, z, t]).astype(jnp.int32)
+    x = layer_input[0]
+    tokens = x.shape[0] // 2
+    model = x.shape[1]
+    heads = model // HD
+    pairs = heads // 2
+    quads = heads // 4
+    quad = 4 * HD
+    rows, width, owidth = w_up.shape[0], w_up.shape[1], w_out.shape[1]
+    hidden = 2 * width
+    length = 2 * tokens
+    scale = 1.0 / math.sqrt(HD)
+
+    own = lambda v: lax.dynamic_slice_in_dim(v, t * tokens, tokens)
+    other = lambda v: lax.dynamic_slice_in_dim(v, (1 - t) * tokens, tokens)
+    xt = own(x)
+
+    wq_arrays, wq_layout = gather_pieces(w_qkv.transpose(1, 0, 2), ctx, ("tensor", "y"), 1)
+    ring = [xt]
+    for _ in range(1, ctx):
+        ring.append(shift(ring[-1], 1, ctx))
+    sides = [other(x)] + [swap(v, "tensor") for v in ring[1:]]
+    up_arrays, up_layout = gather_pieces(w_up, ctx, ("y", "tensor"), 0)
+    down_arrays, down_layout = gather_pieces(
+        jnp.concatenate([w_down, w_out], 1), ctx, ("tensor", "y"), 0
+    )
+
+    seg = segments[0].reshape(ctx, 2, tokens)[::-1]
+    seg = lax.dynamic_slice_in_dim(jnp.concatenate([seg, seg]), ctx - 1 - z, ctx)
+    seg = jnp.where(t == 0, seg, seg[:, ::-1])
+    mark = jnp.arange(LANES, dtype=jnp.int32)
+    kmark = jnp.where(
+        (mark < 3) & (seg.reshape(ctx, length)[..., None] != mark), -1e30, 0.0
+    ).astype(BF)
+    qmark = (seg[0, 0][:, None] == mark).astype(BF)
+    qmark = jnp.concatenate([qmark, qmark])
+
+    biases = b_qv.astype(F32)
+    biases_other = swap(biases, "tensor")
+    biases = jnp.where(
+        t == 0,
+        jnp.concatenate([biases, biases_other], 1),
+        jnp.concatenate([biases_other, biases], 1),
+    )
+    bup_mine = b_up.astype(F32)[None]
+    bup_other = swap(bup_mine, "tensor")
+    bup_full = jnp.where(
+        t == 0,
+        jnp.concatenate([bup_mine, bup_other], 1),
+        jnp.concatenate([bup_other, bup_mine], 1),
+    )
+
+    n_pieces = 4 * ctx * 2
+    weights, queries = pl.pallas_call(
+        lambda *refs: prepare_kernel(ctx, rows, owidth, wq_layout, 4, heads, scale, *refs),
+        out_shape=(
+            jax.ShapeDtypeStruct((3, model, model), BF),
+            jax.ShapeDtypeStruct((pairs, length, LANES), BF),
+        ),
+        in_specs=[scalars(), whole((tokens, model)), whole((1, model))] + [anywhere()] * 4,
+        out_specs=(whole((3, model, model)), whole((pairs, length, LANES))),
+        scratch_shapes=[pltpu.SemaphoreType.DMA((n_pieces,))],
+        compiler_params=params(32),
+        name="prepare",
+    )(ids, xt, biases[0:1], *wq_arrays)
+
+    def of_kind(kind):
+        return pl.BlockSpec((None, model, quad), lambda g: (kind, 0, g))
+
+    columns = pl.BlockSpec((length, quad), lambda g: (0, g))
+    rows_t = pl.BlockSpec((quad, length), lambda g: (g, 0))
+    row = pl.BlockSpec((1, quad), lambda g: (0, g))
+    by_pair = lambda *tail: pl.BlockSpec((2,) + tail, lambda g: (g,) + (0,) * len(tail))
+
+    kv = []
+    carry = ()
+    state_shapes = (
+        jax.ShapeDtypeStruct((pairs, 1, length), F32),
+        jax.ShapeDtypeStruct((pairs, LANES + 16, length), F32),
+    )
+    state_specs = (by_pair(1, length), by_pair(LANES + 16, length))
+    for r in range(ctx):
+        first = r == 0
+        k_r, v_r, kt_r, *carry = pl.pallas_call(
+            lambda *refs, first=first: attend_kernel(first, *refs),
+            grid=(quads,),
+            out_shape=(
+                jax.ShapeDtypeStruct((length, model), BF),
+                jax.ShapeDtypeStruct((length, model), BF),
+                jax.ShapeDtypeStruct((model, length), BF),
+            ) + state_shapes,
+            in_specs=[
+                whole((tokens, model)), whole((tokens, model)), of_kind(1), of_kind(2), row,
+                by_pair(length, LANES), whole((length, LANES)), whole((length, LANES)),
+            ] + ([] if first else list(state_specs)),
+            out_specs=(columns, columns, rows_t) + state_specs,
+            compiler_params=params(40),
+            name="attend",
+        )(ring[r], sides[r], weights, weights, biases[1:2], queries, qmark, kmark[r], *carry)
+        kv.append((k_r, v_r, kt_r))
+    top, sums = carry
+
+    vec = jnp.stack(
+        [b_out, ln1_gain, ln1_bias, b_down, ln2_gain, ln2_bias, ln2_bias, ln2_bias]
+    ).astype(F32)
+    sds = jax.ShapeDtypeStruct
+    mid_shapes = (
+        sds((tokens, model), BF), sds((tokens, model), F32), sds((pairs, length, LANES), BF),
+        sds((pairs, 1, length), F32), sds((pairs, 1, length), F32), sds((8, model), F32),
+        sds((1, hidden), F32), sds((tokens, hidden), BF), sds((tokens, hidden), BF),
+        sds((tokens, model), BF), sds((tokens, model), BF), sds((tokens, model), BF),
+        sds((tokens, model), BF),
+    )
+    (out_own, dz1, dos, lse, delta, vgrads, gup_bias, u, dpb, h1b, dmb, dzb, ob) = pl.pallas_call(
+        lambda *refs: middle_kernel(ctx, rows, up_layout, down_layout, down_layout, 4, 4, heads, *refs),
+        out_shape=mid_shapes,
+        in_specs=[
+            scalars(), whole(sums.shape), whole(top.shape), whole((tokens, model)),
+            whole((tokens, model)), whole((8, model)), whole((1, hidden)),
+        ] + [anywhere()] * 8,
+        out_specs=tuple(whole(s.shape) for s in mid_shapes),
+        scratch_shapes=[
+            pltpu.VMEM((model, hidden), BF), pltpu.VMEM((model, hidden), BF),
+            pltpu.VMEM((model, model), BF), pltpu.VMEM((tokens, hidden), F32),
+            pltpu.VMEM((tokens, model), F32),
+            pltpu.SemaphoreType.DMA((n_pieces,)), pltpu.SemaphoreType.DMA((n_pieces,)),
+            pltpu.SemaphoreType.DMA((n_pieces,)),
+        ],
+        compiler_params=params(56),
+        name="middle",
+    )(ids, sums, top, xt, own(cotangent[0]), vec, bup_full, *up_arrays, *down_arrays)
+
+    up_order, down_order, qkv_order = ("y", "tensor"), ("tensor", "y"), ("y", "tensor")
+    lay_up = scatter_layout(ctx, rows, up_order, 0)
+    lay_down = scatter_layout(ctx, rows, down_order, 0)
+    piece = lambda w: sds((2, 2, ctx * rows, w), BF)
+    chunk = pl.BlockSpec((tokens, model), lambda c: (0, c))
+    up0, up1, down0, down1 = pl.pallas_call(
+        lambda *refs: feed_grads_kernel(ctx, rows, lay_up, lay_down, lay_down, *refs),
+        grid=(hidden // model,),
+        out_shape=(piece(width), piece(width), piece(width + owidth), piece(width + owidth)),
+        in_specs=[scalars()] + [whole((tokens, model))] * 4 + [chunk, chunk],
+        out_specs=(anywhere(),) * 4,
+        scratch_shapes=[
+            pltpu.VMEM((model, hidden), BF), pltpu.VMEM((model, hidden), BF),
+            pltpu.VMEM((model, model), BF), pltpu.VMEM((model, tokens), BF),
+            pltpu.VMEM((model, tokens), BF),
+            pltpu.SemaphoreType.DMA((n_pieces,)), pltpu.SemaphoreType.DMA((n_pieces,)),
+            pltpu.SemaphoreType.DMA((n_pieces,)),
+        ],
+        compiler_params=params(40),
+        name="feed_grads",
+    )(ids, h1b, dmb, dzb, ob, u, dpb)
+    grad_up = scatter_sum(up0, up1, ctx, rows, up_order, 0)
+    grad_down = scatter_sum(down0, down1, ctx, rows, down_order, 0)
+
+    dkv, gbv, arrived = [None] * ctx, None, []
+    dqt = ()
+    own_part = None
+    for i, r in enumerate(list(range(1, ctx)) + [0]):
+        first = i == 0
+        k_r, v_r, kt_r = kv[r]
+        dk_r, dv_r, acc, gbv_r, dxa, dxb = pl.pallas_call(
+            lambda *refs, first=first: attend_back_kernel(first, *refs),
+            grid=(quads,),
+            out_shape=(
+                sds((length, model), BF), sds((length, model), BF), sds((pairs, LANES, length), F32),
+                sds((1, model), F32), sds((tokens, model), BF), sds((tokens, model), BF),
+            ),
+            in_specs=[
+                columns, columns, rows_t, by_pair(length, LANES), whole((length, LANES)),
+                whole((length, LANES)), by_pair(length, LANES), by_pair(1, length), by_pair(1, length),
+                of_kind(1), of_kind(2),
+            ] + ([] if first else [by_pair(LANES, length)]),
+            out_specs=(
+                columns, columns, by_pair(LANES, length), row, whole((tokens, model)), whole((tokens, model)),
+            ),
+            scratch_shapes=[pltpu.VMEM((length, model), F32)],
+            compiler_params=params(40),
+            name="attend_back",
+        )(k_r, v_r, kt_r, queries, qmark, kmark[r], dos, lse, delta, weights, weights, *dqt)
+        dqt = (acc,)
+        dkv[r] = (dk_r, dv_r)
+        gbv = gbv_r if gbv is None else gbv + gbv_r
+        part = add(dxa, swap(dxb, "tensor"))
+        if r == 0:
+            own_part = part
+        else:
+            arrived.append(shift(part.astype(BF), -r, ctx))
+
+    lay_qkv = scatter_layout(ctx, rows, qkv_order, 1)
+    piece = sds((2, 2, 3, ctx * rows, owidth), BF)
+    dxq, gbq, qkv0, qkv1 = pl.pallas_call(
+        lambda *refs: last_kernel(ctx, rows, lay_qkv, scale, *refs),
+        grid=(quads,),
+        out_shape=(sds((tokens, model), F32), sds((1, model), F32), piece, piece),
+        in_specs=[scalars(), by_pair(LANES, length), of_kind(0)]
+        + [whole((tokens, model))] * (2 * ctx) + [columns] * (2 * ctx),
+        out_specs=(whole((tokens, model)), row, anywhere(), anywhere()),
+        scratch_shapes=[
+            pltpu.VMEM((3, model, model), BF), pltpu.VMEM((2 * ctx, model, tokens), BF),
+            pltpu.VMEM((tokens, model), F32), pltpu.SemaphoreType.DMA((n_pieces,)),
+        ],
+        compiler_params=params(48),
+        name="last",
+    )(ids, dqt[0], weights, *[v for pair in zip(ring, sides) for v in pair],
+      *[d[0] for d in dkv], *[d[1] for d in dkv])
+
+    grad_in = dz1 + dxq + own_part
+    for v in arrived:
+        grad_in = grad_in + v.astype(F32)
+    grad_qkv = scatter_sum(qkv0, qkv1, ctx, rows, qkv_order, 1).transpose(1, 0, 2)
+
+    vectors = jnp.concatenate([gbq[0], gbv[0], vgrads.reshape(-1), gup_bias[0]])
+    vectors = sum_everywhere(vectors.reshape(-1, LANES), ctx).reshape(-1)
+    pick = lambda i: vectors[i * model : (i + 1) * model]
+    part_of = lambda v, w: lax.dynamic_slice_in_dim(v, t * w, w)
+    grad_bqv = jnp.stack([part_of(pick(0), owidth), part_of(pick(1), owidth)])
+
+    def both_halves(mine):
+        theirs = swap(mine, "tensor")
+        return jnp.where(
+            t == 0, jnp.concatenate([mine, theirs]), jnp.concatenate([theirs, mine])
+        )[None]
+
+    return (
+        both_halves(out_own),
+        both_halves(grad_in.astype(BF)).astype(F32),
+        grad_qkv,
+        grad_bqv,
+        grad_down[:, width:],
+        pick(2),
+        pick(3),
+        pick(4),
+        grad_up,
+        part_of(vectors[10 * model :], width),
+        grad_down[:, :width],
+        pick(5),
+        pick(6),
+        pick(7),
+    )
 
 
 neg_large = -1e30
 
 
-def layer_norm(summed, gain, bias):
+def general_norm(summed, gain, bias):
     centred = summed - jnp.mean(summed, -1, keepdims=True)
     scaling = lax.rsqrt(jnp.mean(centred * centred, -1, keepdims=True) + 1e-05)
     normal_part = centred * scaling
     return (normal_part * gain + bias, normal_part, scaling)
 
 
-def norm_back(upstream, normal_part, scaling, gain):
+def general_back(upstream, normal_part, scaling, gain):
     scaled = upstream * gain
     inner = (
         scaled
@@ -37,7 +688,7 @@
     )
 
 
-def on_device(
+def general(
     layer_input,
     segments,
     w_qkv,
@@ -127,7 +778,7 @@
     ) + b_out.astype(jnp.float32)
     first_gain = ln1_gain.astype(jnp.float32)
     second_gain = ln2_gain.astype(jnp.float32)
-    hidden, first_normal, first_scale = layer_norm(
+    hidden, first_normal, first_scale = general_norm(
         inputs.astype(jnp.float32) + branch, first_gain, ln1_bias.astype(jnp.float32)
     )
     hidden_low = hidden.astype(jnp.bfloat16)
@@ -139,7 +790,7 @@
     second_branch = lax.psum(second_part.astype(jnp.bfloat16), "tensor").astype(
         jnp.float32
     ) + b_down.astype(jnp.float32)
-    result, second_normal, second_scale = layer_norm(
+    result, second_normal, second_scale = general_norm(
         hidden + second_branch, second_gain, ln2_bias.astype(jnp.float32)
     )
     qkv_full, out_full, up_full, down_full = (
@@ -149,7 +800,7 @@
         lax.all_gather(w_down, ("shard", "ctx"), axis=0, tiled=True),
     )
     upstream = cotangent[0].astype(jnp.float32)
-    second_grad, grad_gain_two, grad_bias_two = norm_back(
+    second_grad, grad_gain_two, grad_bias_two = general_back(
         upstream, second_normal, second_scale, second_gain
     )
     grad_down_bias = jnp.sum(second_grad, 0)
@@ -164,7 +815,7 @@
     hidden_grad = second_grad + lax.psum(hidden_part.astype(jnp.bfloat16), "tensor").astype(
         jnp.float32
     )
-    first_grad, grad_gain_one, grad_bias_one = norm_back(
+    first_grad, grad_gain_one, grad_bias_one = general_back(
         hidden_grad, first_normal, first_scale, first_gain
     )
     grad_out_bias = jnp.sum(first_grad, 0)
@@ -263,41 +914,28 @@
 
 
 def solution(mesh):
+    sizes = dict(mesh.shape)
+    ctx = sizes["ctx"]
+    fits = sizes["shard"] == 4 and sizes["tensor"] == 2 and ctx & (ctx - 1) == 0
+    if fits:
+        mesh = Mesh(mesh.devices.reshape(2, 2, ctx, 2), EVERY)
+        shard, body = ("y", "core"), on_device
+        rows = ("y", "core", "ctx")
+    else:
+        shard, body = "shard", general
+        rows = ("shard", "ctx")
+    activations, matrix = P(shard, "ctx", None), P(rows, "tensor")
+    cube, pair = P(rows, None, "tensor"), P(None, "tensor")
     return jax.shard_map(
-        on_device,
+        body,
         mesh=mesh,
         in_specs=(
-            P("shard", "ctx", None),
-            P("shard", None),
-            P(("shard", "ctx"), None, "tensor"),
-            P(None, "tensor"),
-            P(("shard", "ctx"), "tensor"),
-            P(),
-            P(),
-            P(),
-            P(("shard", "ctx"), "tensor"),
-            P("tensor"),
-            P(("shard", "ctx"), "tensor"),
-            P(),
-            P(),
-            P(),
-            P("shard", "ctx", None),
+            activations, P(shard, None), cube, pair, matrix, P(), P(), P(), matrix, P("tensor"),
+            matrix, P(), P(), P(), activations,
         ),
         out_specs=(
-            P("shard", "ctx", None),
-            P("shard", "ctx", None),
-            P(("shard", "ctx"), None, "tensor"),
-            P(None, "tensor"),
-            P(("shard", "ctx"), "tensor"),
-            P(),
-            P(),
-            P(),
-            P(("shard", "ctx"), "tensor"),
-            P("tensor"),
-            P(("shard", "ctx"), "tensor"),
-            P(),
-            P(),
-            P(),
+            activations, activations, cube, pair, matrix, P(), P(), P(), matrix, P("tensor"),
+            matrix, P(), P(), P(),
         ),
         check_vma=False,
     )

time: 918 us -> 459 us (0.50)
  waiting for transfers between devices: 572 us -> 208 us
  matrix products: 128 us -> 0 us
  blocking collectives: 111 us -> 0 us
  Pallas kernels: 0 us -> 91.5 us
  starting transfers between devices: 1.25 us -> 76.5 us
  other arithmetic: 38.6 us -> 20.9 us
  between operations: 15.8 us -> 2.64 us
    reduce_scatter x5 -> x0, waiting for transfers between devices: 284 us -> none  [the longest x1 79.4 us: on_device(): lax.psum_scatter(grad_down, ('shard', 'ctx'), scatter_dimension=0, tiled=...]
    ppermute x0 -> x61, waiting for transfers between devices: none -> 208 us  [the longest x35 139 us: swap(): return lax.ppermute(v, axis, SWAP)]
    dot_general x40 -> x0, matrix products: 128 us -> none  [the longest x4 21.3 us: score_grads(): jnp.einsum('htk,htd->khd', probs.astype(jnp.bfloat16), grad_heads, prefer...]
    all_gather x5 -> x0, waiting for transfers between devices: 126 us -> none  [the longest x1 45.4 us: on_device(): lax.all_gather(w_qkv, ('shard', 'ctx'), axis=0, tiled=True)]
    psum x4 -> x0, waiting for transfers between devices: 97.5 us -> none  [the longest x1 34.2 us: on_device(): lax.psum(hidden_part.astype(jnp.bfloat16), 'tensor').astype(jnp.float32)]
    pallas_call x0 -> x12, Pallas kernels: none -> 91.5 us  [the longest x4 27.1 us: on_device(): pl.pallas_call(lambda *refs, first=first: attend_back_kernel(first, *refs...]
    ppermute x0 -> x61, starting transfers between devices: none -> 76.5 us  [the longest x24 45.7 us: shift(): return lax.ppermute(v, 'ctx', [(i, (i + by) % ctx) for i in range(ctx)])]
    unnamed x16 -> x0, waiting for transfers between devices: 64.7 us -> none
  transfers between devices with their start and end apart: 15 -> 61, of which waited for: 12 -> 27; matrix products, arithmetic and copies ran while one was open for 9% -> 8% of each run, Pallas kernels for 0% -> 8%
where the time goes in v1:
time: 459 us; the launch traced here: 450 us
  waiting for transfers between devices  208 us (45%)
  Pallas kernels  91.5 us (20%)
  starting transfers between devices  76.5 us (17%)
  local copies, waits for them, and re-layouts  50.2 us (11%)
  other arithmetic  20.9 us (5%)
    ppermute x35, waiting for transfers between devices, swap(): return lax.ppermute(v, axis, SWAP)  139 us
    ppermute x24, waiting for transfers between devices, shift(): return lax.ppermute(v, 'ctx', [(i, (i + by) % ctx) for i in range(ctx)])  65.5 us
    ppermute x24, starting transfers between devices, shift(): return lax.ppermute(v, 'ctx', [(i, (i + by) % ctx) for i in range(ctx)])  45.7 us
    unnamed x250, local copies, waits for them, and re-layouts  39.5 us
    ppermute x35, starting transfers between devices, swap(): return lax.ppermute(v, axis, SWAP)  29.2 us
    pallas_call x4, Pallas kernels, on_device(): pl.pallas_call(lambda *refs, first=first: attend_back_kernel(first, *refs...  27.1 us
    pallas_call x4, Pallas kernels, on_device(): pl.pallas_call(lambda *refs, first=first: attend_kernel(first, *refs), gr...  22.1 us
    pallas_call x1, Pallas kernels, on_device(): pl.pallas_call(lambda *refs: middle_kernel(ctx, rows, up_layout, down_lay...  17.1 us
  transfers between devices with their start and end apart: 61, of which 27 were waited for; matrix products, arithmetic and copies ran while one was open for 8% of the time, Pallas kernels for 8%

profile of v1, /device:TPU:0, one launch (start us, length us, event | category | flops | bytes accessed | tf_op | source)
XLA Modules:
  0.0 449.8 jit_solution(11723002278539654031)
XLA Ops:
  0.7 3.1 collective-permute-start.5
  3.8 2.6 collective-permute-start.6
  7.7 1.6 constant_dynamic-update-slice_fusion.11
  9.3 1.4 constant_dynamic-update-slice_fusion.10
  14.0 1.6 constant_dynamic-update-slice_fusion.9
  16.4 3.4 collective-permute-start.15
  20.0 2.4 collective-permute-start.17
  24.2 2.6 collective-permute-done.15
  26.8 6.7 %collective-permute-start.24 = (bf16[48,1920]{1,0:T(8,128)(2,1)S(1)}, bf16[48,1920]{1,0:T(8,128)(2,1)S(1)}, u32[]{:S(2)}, u32[]{:S(2)}) collective-permute-start(bf16[48,1920]{1,0:T(8,128)(2,1)S(1)} %get-tuple-element.179), channel_id=1, source_target_pairs={{0,6},{2,0},{4,2},{6,4},{1,7},{3,1},{5,3},{7,5},{8,14},{10,8},{12,... | collective-permute-start | bytes 552968 | tf_op jit(solution)/shard_map/ppermute | solution.py:345
  33.6 4.1 collective-permute-done.16
  37.6 1.5 collective-permute-start.4
  39.2 1.6 collective-permute-done.17
  40.7 4.5 %collective-permute-start = (bf16[256,768]{1,0:T(8,128)(2,1)S(1)}, bf16[256,768]{1,0:T(8,128)(2,1)S(1)}, u32[]{:S(2)}, u32[]{:S(2)}) collective-permute-start(bf16[256,768]{1,0:T(8,128)(2,1)S(1)} %get-tuple-element.155.refs_1_.refs_0_.refs_3_), channel_id=1, source_target_pairs={{0,2},{2,4},{4,6},{6,0},{1,3},{3,5},{5,7},{7,1},{8,10},{10,12},{12... | collective-permute-start | bytes 1179656 | tf_op jit(solution)/shard_map/ppermute | solution.py:345
  46.2 1.5 collective-permute-start.18
  48.8 1.9 collective-permute-start.25
  53.4 3.3 collective-permute-done.refs_0_.refs_5_
  56.7 15.2 %collective-permute-done.25 = bf16[192,1920]{1,0:T(8,128)(2,1)S(1)} collective-permute-done((bf16[192,1920]{1,0:T(8,128)(2,1)S(1)}, bf16[192,1920]{1,0:T(8,128)(2,1)S(1)}, u32[]{:S(2)}, u32[]{:S(2)}) %collective-permute-start.25) | collective-permute-done | bytes 737312 | tf_op jit(solution)/shard_map/ppermute | solution.py:349
  72.9 1.5 collective-permute-start.26
  76.6 1.5 collective-permute-start.14
  78.7 1.5 collective-permute-start.12
  80.3 7.1 %collective-permute-done.14 = f32[1,1536]{1,0:T(1,128)S(1)} collective-permute-done((f32[1,1536]{1,0:T(1,128)S(1)}, f32[1,1536]{1,0:T(1,128)S(1)}, u32[]{:S(2)}, u32[]{:S(2)}) %collective-permute-start.14) | collective-permute-done | bytes 6176 | tf_op jit(solution)/shard_map/ppermute | solution.py:349
  89.3 27.6 %collective-permute-done.12.refs_1_.refs_8_ = bf16[256,768]{1,0:T(8,128)(2,1)S(1)} collective-permute-done((bf16[256,768]{1,0:T(8,128)(2,1)S(1)}, bf16[256,768]{1,0:T(8,128)(2,1)S(1)}, u32[]{:S(2)}, u32[]{:S(2)}) %collective-permute-start.12) | collective-permute-done | bytes 393248 | tf_op jit(solution)/shard_map/ppermute | solution.py:349
  118.2 8.5 %collective-permute-done.2.refs_0_.refs_9_ = bf16[256,768]{1,0:T(8,128)(2,1)} collective-permute-done((bf16[256,768]{1,0:T(8,128)(2,1)S(1)}, bf16[256,768]{1,0:T(8,128)(2,1)}, u32[]{:S(2)}, u32[]{:S(2)}) %collective-permute-start.2) | collective-permute-done | bytes 393248 | tf_op jit(solution)/shard_map/ppermute | solution.py:345
  129.9 1.6 collective-permute-done.11.refs_6_
  135.1 3.3 prepare.1
  138.6 5.2 %attend.4 = (bf16[512,768]{1,0:T(8,128)(2,1)S(1)}, bf16[512,768]{1,0:T(8,128)(2,1)S(1)}, bf16[768,512]{1,0:T(8,128)(2,1)S(1)}, f32[6,1,512]{2,1,0:T(1,128)S(1)}, f32[6,144,512]{2,1,0:T(8,128)S(1)}) custom-call(bf16[256,768]{1,0:T(8,128)(2,1)S(1)} %copy-done.10, bf16[256,768]{1,0:T(8,128)(2,1)S(1)} %copy-done.12, ...), custom_call_target="tpu_custom_call" | custom-call | tf_op jit(solution)/shard_map/attend/pallas_call | solution.py:500
  143.8 5.2 %attend.5 = (bf16[512,768]{1,0:T(8,128)(2,1)S(1)}, bf16[512,768]{1,0:T(8,128)(2,1)S(1)}, bf16[768,512]{1,0:T(8,128)(2,1)S(1)}, f32[6,1,512]{2,1,0:T(1,128)S(1)}, f32[6,144,512]{2,1,0:T(8,128)S(1)}) custom-call(bf16[256,768]{1,0:T(8,128)(2,1)S(1)} %copy-done.18, bf16[256,768]{1,0:T(8,128)(2,1)S(1)} %copy-done.24, ...), custom_call_target="tpu_custom_call" | custom-call | tf_op jit(solution)/shard_map/attend/pallas_call | solution.py:500
  149.1 5.2 %attend.6 = (bf16[512,768]{1,0:T(8,128)(2,1)S(1)}, bf16[512,768]{1,0:T(8,128)(2,1)S(1)}, bf16[768,512]{1,0:T(8,128)(2,1)S(1)}, f32[6,1,512]{2,1,0:T(1,128)S(1)}, f32[6,144,512]{2,1,0:T(8,128)S(1)}) custom-call(bf16[256,768]{1,0:T(8,128)(2,1)S(1)} %copy-done.21, bf16[256,768]{1,0:T(8,128)(2,1)S(1)} %copy-done.27, ...), custom_call_target="tpu_custom_call" | custom-call | tf_op jit(solution)/shard_map/attend/pallas_call | solution.py:500
  156.2 6.6 %attend.7 = (bf16[512,768]{1,0:T(8,128)(2,1)S(1)}, bf16[512,768]{1,0:T(8,128)(2,1)S(1)}, bf16[768,512]{1,0:T(8,128)(2,1)S(1)}, f32[6,1,512]{2,1,0:T(1,128)S(1)}, f32[6,144,512]{2,1,0:T(8,128)S(1)}) custom-call(bf16[256,768]{1,0:T(8,128)(2,1)} %collective-permute-done.2.refs_0_.refs_9_, bf16[256,768]{1,0:T(8,128)(2,1)S(1)} %collective-permute-done.3.refs_1_.refs_10_, ...), custom_call_target="tpu_custom_call" | custom-call | tf_op jit(solution)/shard_map/attend/pallas_call | solution.py:500
  167.4 17.1 %middle.1 = (bf16[256,768]{1,0:T(8,128)(2,1)}, f32[256,768]{1,0:T(8,128)}, bf16[6,512,128]{2,1,0:T(8,128)(2,1)}, f32[6,1,512]{2,1,0:T(1,128)}, f32[6,1,512]{2,1,...) custom-call(s32[4]{0:T(128)} %copy-done.88, ...), custom_call_target="tpu_custom_call" | custom-call | tf_op jit(solution)/shard_map/middle/pallas_call | solution.py:530
  194.8 6.7 %attend_back.4 = (bf16[512,768]{1,0:T(8,128)(2,1)S(1)}, bf16[512,768]{1,0:T(8,128)(2,1)S(1)}, f32[6,128,512]{2,1,0:T(8,128)S(1)}, f32[1,768]{1,0:T(1,128)S(1)}, ...) custom-call(bf16[512,768]{1,0:T(8,128)(2,1)S(1)} %copy-done.43, bf16[512,768]{1,0:T(8,128)(2,1)S(1)} %copy-done.45, ...), custom_call_target="tpu_custom_call" | custom-call | tf_op jit(solution)/shard_map/attend_back/pallas_call | solution.py:579
  203.2 6.9 %attend_back.5 = (bf16[512,768]{1,0:T(8,128)(2,1)S(1)}, bf16[512,768]{1,0:T(8,128)(2,1)S(1)}, f32[6,128,512]{2,1,0:T(8,128)S(1)}, f32[1,768]{1,0:T(1,128)S(1)}, ...) custom-call(bf16[512,768]{1,0:T(8,128)(2,1)S(1)} %copy-done.69, bf16[512,768]{1,0:T(8,128)(2,1)S(1)} %copy-done.71, ...), custom_call_target="tpu_custom_call" | custom-call | tf_op jit(solution)/shard_map/attend_back/pallas_call | solution.py:579
  211.8 6.8 %attend_back.6 = (bf16[512,768]{1,0:T(8,128)(2,1)S(1)}, bf16[512,768]{1,0:T(8,128)(2,1)S(1)}, f32[6,128,512]{2,1,0:T(8,128)S(1)}, f32[1,768]{1,0:T(1,128)S(1)}, ...) custom-call(bf16[512,768]{1,0:T(8,128)(2,1)S(1)} %copy-done.63, bf16[512,768]{1,0:T(8,128)(2,1)S(1)} %copy-done.65, ...), custom_call_target="tpu_custom_call" | custom-call | tf_op jit(solution)/shard_map/attend_back/pallas_call | solution.py:579
  221.1 6.7 %attend_back.7 = (bf16[512,768]{1,0:T(8,128)(2,1)S(1)}, bf16[512,768]{1,0:T(8,128)(2,1)S(1)}, f32[6,128,512]{2,1,0:T(8,128)S(1)}, f32[1,768]{1,0:T(1,128)S(1)}, ...) custom-call(bf16[512,768]{1,0:T(8,128)(2,1)S(1)} %copy-done.57, bf16[512,768]{1,0:T(8,128)(2,1)S(1)} %copy-done.59, ...), custom_call_target="tpu_custom_call" | custom-call | tf_op jit(solution)/shard_map/attend_back/pallas_call | solution.py:579
  230.0 12.5 %last.1 = (f32[256,768]{1,0:T(8,128)S(1)}, f32[1,768]{1,0:T(1,128)S(1)}, bf16[2,2,3,192,384]{4,3,2,1,0:T(8,128)(2,1)}, bf16[2,2,3,192,384]{4,3,2,1,0:T(8,128)(2,1)}) custom-call(s32[4]{0:T(128)S(1)} %copy-done.89, f32[6,128,512]{2,1,0:T(8,128)} %copy-done.31, bf16[3,768,768]{2,1,0:T(8,128)(2,1)} %copy-done.2, bf16[256,768]{1,0:T(8,128)(2,1)S(1)} %copy-done.11, ...), custom_call_target="tpu_custom_call" | custom-call | tf_op jit(solution)/shard_map/last/pallas_call | solution.py:609
  250.9 2.2 collective-permute-done.45
  254.5 3.6 collective-permute-done.46
  258.1 4.0 collective-permute-done.47
  262.8 1.6 collective-permute-start.48
  267.4 9.2 %feed_grads.1 = (bf16[2,2,192,1536]{3,2,1,0:T(8,128)(2,1)S(1)}, bf16[2,2,192,1536]{3,2,1,0:T(8,128)(2,1)S(1)}, bf16[2,2,192,1920]{3,2,1,0:T(8,128)(2,1)S(1)}, bf16[2,2,192,1920]{3,2,1,0:T(8,128)(2,1)}) custom-call(s32[4]{0:T(128)S(1)} %copy-done.89, bf16[256,768]{1,0:T(8,128)(2,1)S(1)} %copy-done.74, bf16[256,768]{1,0:T(8,128)(2,1)S(1)} %copy-done.75, ...), custom_call_target="tpu_custom_call" | custom-call | tf_op jit(solution)/shard_map/feed_grads/pallas_call | solution.py:554
  277.2 1.5 collective-permute-start.30
  280.8 1.6 collective-permute-start.35
  283.5 14.1 %collective-permute-done.33 = bf16[256,768]{1,0:T(8,128)(2,1)S(1)} collective-permute-done((bf16[256,768]{1,0:T(8,128)(2,1)S(1)}, bf16[256,768]{1,0:T(8,128)(2,1)S(1)}, u32[]{:S(2)}, u32[]{:S(2)}) %collective-permute-start.33) | collective-permute-done | bytes 393248 | tf_op jit(solution)/shard_map/ppermute | solution.py:349
  297.6 1.5 collective-permute-start.29
  299.2 6.8 %collective-permute-done.35 = bf16[256,768]{1,0:T(8,128)(2,1)S(1)} collective-permute-done((bf16[256,768]{1,0:T(8,128)(2,1)S(1)}, bf16[256,768]{1,0:T(8,128)(2,1)S(1)}, u32[]{:S(2)}, u32[]{:S(2)}) %collective-permute-start.35) | collective-permute-done | bytes 393248 | tf_op jit(solution)/shard_map/ppermute | solution.py:349
  306.9 1.4 collective-permute-start.34
  308.3 5.3 %collective-permute-done.29 = bf16[256,768]{1,0:T(8,128)(2,1)S(1)} collective-permute-done((bf16[256,768]{1,0:T(8,128)(2,1)S(1)}, bf16[256,768]{1,0:T(8,128)(2,1)S(1)}, u32[]{:S(2)}, u32[]{:S(2)}) %collective-permute-start.29) | collective-permute-done | bytes 393248 | tf_op jit(solution)/shard_map/ppermute | solution.py:349
  317.7 23.0 %collective-permute-done.34 = bf16[256,768]{1,0:T(8,128)(2,1)S(1)} collective-permute-done((bf16[256,768]{1,0:T(8,128)(2,1)S(1)}, bf16[256,768]{1,0:T(8,128)(2,1)S(1)}, u32[]{:S(2)}, u32[]{:S(2)}) %collective-permute-start.34) | collective-permute-done | bytes 393248 | tf_op jit(solution)/shard_map/ppermute | solution.py:345
  341.1 1.6 collective-permute-start.37
  344.5 1.6 collective-permute-start.56
  346.2 19.7 %collective-permute-done.39 = bf16[2,3,192,384]{3,2,1,0:T(8,128)(2,1)S(1)} collective-permute-done((bf16[2,3,192,384]{3,2,1,0:T(8,128)(2,1)S(1)}, bf16[2,3,192,384]{3,2,1,0:T(8,128)(2,1)S(1)}, u32[]{:S(2)}, u32[]{:S(2)}) %collective-permute-start.39) | collective-permute-done | bytes 884768 | tf_op jit(solution)/shard_map/ppermute | solution.py:349
  369.0 10.3 %collective-permute-done.40 = bf16[3,192,384]{2,1,0:T(8,128)(2,1)S(1)} collective-permute-done((bf16[3,192,384]{2,1,0:T(8,128)(2,1)S(1)}, bf16[3,192,384]{2,1,0:T(8,128)(2,1)S(1)}, u32[]{:S(2)}, u32[]{:S(2)}) %collective-permute-start.40) | collective-permute-done | bytes 442400 | tf_op jit(solution)/shard_map/ppermute | solution.py:349
  379.5 1.7 collective-permute-start.42
  381.1 1.9 collective-permute-start.43
  383.1 1.4 fusion.10
  385.4 2.4 collective-permute-done.43
  390.0 18.5 %collective-permute-done.50 = bf16[2,192,1920]{2,1,0:T(8,128)(2,1)S(1)} collective-permute-done((bf16[2,192,1920]{2,1,0:T(8,128)(2,1)S(1)}, bf16[2,192,1920]{2,1,0:T(8,128)(2,1)S(1)}, u32[]{:S(2)}, u32[]{:S(2)}) %collective-permute-start.50) | collective-permute-done | bytes 1474592 | tf_op jit(solution)/shard_map/ppermute | solution.py:349
  409.4 5.4 %collective-permute-done.57 = bf16[192,1536]{1,0:T(8,128)(2,1)S(1)} collective-permute-done((bf16[192,1536]{1,0:T(8,128)(2,1)S(1)}, bf16[192,1536]{1,0:T(8,128)(2,1)S(1)}, u32[]{:S(2)}, u32[]{:S(2)}) %collective-permute-start.57) | collective-permute-done | bytes 589856 | tf_op jit(solution)/shard_map/ppermute | solution.py:349
  415.1 6.9 %collective-permute-start.59 = (bf16[48,1536]{1,0:T(8,128)(2,1)S(1)}, bf16[48,1536]{1,0:T(8,128)(2,1)S(1)}, u32[]{:S(2)}, u32[]{:S(2)}) collective-permute-start(bf16[48,1536]{1,0:T(8,128)(2,1)S(1)} %get-tuple-element.161), channel_id=1, source_target_pairs={{0,4},{2,6},{4,0},{6,2},{1,5},{3,7},{5,1},{7,3},{8,12},{10,14},{12... | collective-permute-start | bytes 442376 | tf_op jit(solution)/shard_map/ppermute | solution.py:345
  422.0 1.9 collective-permute-start.60
  424.2 1.9 collective-permute-start.52
  426.9 2.9 collective-permute-start.54
  429.8 13.1 %collective-permute-done.59 = bf16[48,1536]{1,0:T(8,128)(2,1)S(1)} collective-permute-done((bf16[48,1536]{1,0:T(8,128)(2,1)S(1)}, bf16[48,1536]{1,0:T(8,128)(2,1)S(1)}, u32[]{:S(2)}, u32[]{:S(2)}) %collective-permute-start.59) | collective-permute-done | bytes 147488 | tf_op jit(solution)/shard_map/ppermute | solution.py:345
  443.7 4.2 collective-permute-done.53
  (401 shorter events, 85.5 us)
Async XLA Ops:
  0.6 126.6 %copy-start = (bf16[1,512,768]{2,1,0:T(8,128)(2,1)S(1)}, bf16[1,512,768]{2,1,0:T(8,128)(2,1)}, u32[]{:S(2)}) copy-start(bf16[1,512,768]{2,1,0:T(8,128)(2,1)} %param.29) | copy-start | bytes 2359300
  0.7 15.7 %collective-permute-start.5 = (bf16[3,48,384]{2,1,0:T(8,128)(2,1)}, bf16[3,48,384]{2,1,0:T(8,128)(2,1)S(1)}, u32[]{:S(2)}, u32[]{:S(2)}) collective-permute-start(bf16[3,48,384]{2,1,0:T(8,128)(2,1)} %bitcast.94), channel_id=1, source_target_pairs={{0,2},{2,4},{4,6},{6,0},{1,3},{3,5},{5,7},{7,1},{8,10},{10,12},{12... | collective-permute-start | bytes 331784 | tf_op jit(solution)/shard_map/ppermute | solution.py:345
  3.8 16.1 %collective-permute-start.6 = (bf16[3,48,384]{2,1,0:T(8,128)(2,1)}, bf16[3,48,384]{2,1,0:T(8,128)(2,1)S(1)}, u32[]{:S(2)}, u32[]{:S(2)}) collective-permute-start(bf16[3,48,384]{2,1,0:T(8,128)(2,1)} %bitcast.95), channel_id=1, source_target_pairs={{0,4},{2,6},{4,0},{6,2},{1,5},{3,7},{5,1},{7,3},{8,12},{10,14},{12... | collective-permute-start | bytes 331784 | tf_op jit(solution)/shard_map/ppermute | solution.py:345
  6.4 13.6 %collective-permute-start.7 = (bf16[3,48,384]{2,1,0:T(8,128)(2,1)}, bf16[3,48,384]{2,1,0:T(8,128)(2,1)}, u32[]{:S(2)}, u32[]{:S(2)}) collective-permute-start(bf16[3,48,384]{2,1,0:T(8,128)(2,1)} %bitcast.96), channel_id=1, source_target_pairs={{0,6},{2,0},{4,2},{6,4},{1,7},{3,1},{5,3},{7,5},{8,14},{10,8},{12,... | collective-permute-start | bytes 331784 | tf_op jit(solution)/shard_map/ppermute | solution.py:345
  10.7 35.2 %collective-permute-start.22 = (bf16[48,1920]{1,0:T(8,128)(2,1)S(1)}, bf16[48,1920]{1,0:T(8,128)(2,1)S(1)}, u32[]{:S(2)}, u32[]{:S(2)}) collective-permute-start(bf16[48,1920]{1,0:T(8,128)(2,1)S(1)} %get-tuple-element.179), channel_id=1, source_target_pairs={{0,2},{2,4},{4,6},{6,0},{1,3},{3,5},{5,7},{7,1},{8,10},{10,12},{12... | collective-permute-start | bytes 552968 | tf_op jit(solution)/shard_map/ppermute | solution.py:345
  11.4 34.8 %collective-permute-start.23 = (bf16[48,1920]{1,0:T(8,128)(2,1)S(1)}, bf16[48,1920]{1,0:T(8,128)(2,1)S(1)}, u32[]{:S(2)}, u32[]{:S(2)}) collective-permute-start(bf16[48,1920]{1,0:T(8,128)(2,1)S(1)} %get-tuple-element.179), channel_id=1, source_target_pairs={{0,4},{2,6},{4,0},{6,2},{1,5},{3,7},{5,1},{7,3},{8,12},{10,14},{12... | collective-permute-start | bytes 552968 | tf_op jit(solution)/shard_map/ppermute | solution.py:345
  16.4 10.5 %collective-permute-start.15 = (bf16[48,1536]{1,0:T(8,128)(2,1)S(1)}, bf16[48,1536]{1,0:T(8,128)(2,1)S(1)}, u32[]{:S(2)}, u32[]{:S(2)}) collective-permute-start(bf16[48,1536]{1,0:T(8,128)(2,1)S(1)} %copy-done.107), channel_id=1, source_target_pairs={{0,2},{2,4},{4,6},{6,0},{1,3},{3,5},{5,7},{7,1},{8,10},{10,12},{12... | collective-permute-start | bytes 442376 | tf_op jit(solution)/shard_map/ppermute | solution.py:345
  19.8 17.8 %collective-permute-start.16 = (bf16[48,1536]{1,0:T(8,128)(2,1)S(1)}, bf16[48,1536]{1,0:T(8,128)(2,1)S(1)}, u32[]{:S(2)}, u32[]{:S(2)}) collective-permute-start(bf16[48,1536]{1,0:T(8,128)(2,1)S(1)} %copy-done.107), channel_id=1, source_target_pairs={{0,4},{2,6},{4,0},{6,2},{1,5},{3,7},{5,1},{7,3},{8,12},{10,14},{12... | collective-permute-start | bytes 442376 | tf_op jit(solution)/shard_map/ppermute | solution.py:345
  20.0 20.8 %collective-permute-start.17 = (bf16[48,1536]{1,0:T(8,128)(2,1)S(1)}, bf16[48,1536]{1,0:T(8,128)(2,1)S(1)}, u32[]{:S(2)}, u32[]{:S(2)}) collective-permute-start(bf16[48,1536]{1,0:T(8,128)(2,1)S(1)} %copy-done.107), channel_id=1, source_target_pairs={{0,6},{2,0},{4,2},{6,4},{1,7},{3,1},{5,3},{7,5},{8,14},{10,8},{12,... | collective-permute-start | bytes 442376 | tf_op jit(solution)/shard_map/ppermute | solution.py:345
  26.8 20.9 %collective-permute-start.24 = (bf16[48,1920]{1,0:T(8,128)(2,1)S(1)}, bf16[48,1920]{1,0:T(8,128)(2,1)S(1)}, u32[]{:S(2)}, u32[]{:S(2)}) collective-permute-start(bf16[48,1920]{1,0:T(8,128)(2,1)S(1)} %get-tuple-element.179), channel_id=1, source_target_pairs={{0,6},{2,0},{4,2},{6,4},{1,7},{3,1},{5,3},{7,5},{8,14},{10,8},{12,... | collective-permute-start | bytes 552968 | tf_op jit(solution)/shard_map/ppermute | solution.py:345
  37.6 39.0 %collective-permute-start.4 = (f32[2,384]{1,0:T(2,128)S(1)}, f32[2,384]{1,0:T(2,128)S(1)}, u32[]{:S(2)}, u32[]{:S(2)}) collective-permute-start(f32[2,384]{1,0:T(2,128)S(1)} %convert_element_type.163), channel_id=1, source_target_pairs={{0,1},{1,0},{2,3},{3,2},{4,5},{5,4},{6,7},{7,6},{8,9},{9,8},{10,11... | collective-permute-start | bytes 9224 | tf_op jit(solution)/shard_map/ppermute | solution.py:349
  40.7 16.0 %collective-permute-start = (bf16[256,768]{1,0:T(8,128)(2,1)S(1)}, bf16[256,768]{1,0:T(8,128)(2,1)S(1)}, u32[]{:S(2)}, u32[]{:S(2)}) collective-permute-start(bf16[256,768]{1,0:T(8,128)(2,1)S(1)} %get-tuple-element.155.refs_1_.refs_0_.refs_3_), channel_id=1, source_target_pairs={{0,2},{2,4},{4,6},{6,0},{1,3},{3,5},{5,7},{7,1},{8,10},{10,12},{12... | collective-permute-start | bytes 1179656 | tf_op jit(solution)/shard_map/ppermute | solution.py:345
  46.0 32.2 %collective-permute-start.8 = (bf16[3,192,384]{2,1,0:T(8,128)(2,1)S(1)}, bf16[3,192,384]{2,1,0:T(8,128)(2,1)S(1)}, u32[]{:S(2)}, u32[]{:S(2)}) collective-permute-start(bf16[3,192,384]{2,1,0:T(8,128)(2,1)S(1)} %pad_maximum_fusion.2), channel_id=1, source_target_pairs={{0,1},{1,0},{2,3},{3,2},{4,5},{5,4},{6,7},{7,6},{8,9},{9,8},{10,11... | collective-permute-start | bytes 1327112 | tf_op jit(solution)/shard_map/ppermute | solution.py:349
  46.2 28.9 %collective-permute-start.18 = (bf16[192,1536]{1,0:T(8,128)(2,1)S(1)}, bf16[192,1536]{1,0:T(8,128)(2,1)S(1)}, u32[]{:S(2)}, u32[]{:S(2)}) collective-permute-start(bf16[192,1536]{1,0:T(8,128)(2,1)S(1)} %pad_maximum_fusion.1), channel_id=1, source_target_pairs={{0,16},{16,0},{1,17},{17,1},{2,18},{18,2},{3,19},{19,3},{4,20},{20... | collective-permute-start | bytes 1769480 | tf_op jit(solution)/shard_map/ppermute | solution.py:349
  48.8 23.1 %collective-permute-start.25 = (bf16[192,1920]{1,0:T(8,128)(2,1)S(1)}, bf16[192,1920]{1,0:T(8,128)(2,1)S(1)}, u32[]{:S(2)}, u32[]{:S(2)}) collective-permute-start(bf16[192,1920]{1,0:T(8,128)(2,1)S(1)} %pad_maximum_fusion), channel_id=1, source_target_pairs={{0,1},{1,0},{2,3},{3,2},{4,5},{5,4},{6,7},{7,6},{8,9},{9,8},{10,11... | collective-permute-start | bytes 2211848 | tf_op jit(solution)/shard_map/ppermute | solution.py:349
  56.7 21.9 %collective-permute-start.1 = (bf16[256,768]{1,0:T(8,128)(2,1)S(1)}, bf16[256,768]{1,0:T(8,128)(2,1)S(1)}, u32[]{:S(2)}, u32[]{:S(2)}) collective-permute-start(bf16[256,768]{1,0:T(8,128)(2,1)S(1)} %collective-permute-done.refs_0_.refs_5_), channel_id=1, source_target_pairs={{0,2},{2,4},{4,6},{6,0},{1,3},{3,5},{5,7},{7,1},{8,10},{10,12},{12... | collective-permute-start | bytes 1179656 | tf_op jit(solution)/shard_map/ppermute | solution.py:345
  72.9 54.2 %collective-permute-start.26 = (bf16[384,1920]{1,0:T(8,128)(2,1)}, bf16[384,1920]{1,0:T(8,128)(2,1)}, u32[]{:S(2)}, u32[]{:S(2)}) collective-permute-start(bf16[384,1920]{1,0:T(8,128)(2,1)} %constant_dynamic-update-slice_fusion.12.refs_11_), channel_id=1, source_target_pairs={{0,16},{16,0},{1,17},{17,1},{2,18},{18,2},{3,19},{19,3},{4,20},{20... | collective-permute-start | bytes 4423688 | tf_op jit(solution)/shard_map/ppermute | solution.py:349
  75.1 53.6 %copy-start.116 = (bf16[768]{0:T(1024)(128)(2,1)S(1)}, bf16[768]{0:T(1024)(128)(2,1)}, u32[]{:S(2)}) copy-start(bf16[768]{0:T(1024)(128)(2,1)} %param.28) | copy-start | bytes 4612
  75.1 14.0 %collective-permute-start.13 = (bf16[256,768]{1,0:T(8,128)(2,1)S(1)}, bf16[256,768]{1,0:T(8,128)(2,1)S(1)}, u32[]{:S(2)}, u32[]{:S(2)}) collective-permute-start(bf16[256,768]{1,0:T(8,128)(2,1)S(1)} %collective-permute-done.refs_0_.refs_5_), channel_id=1, source_target_pairs={{0,1},{1,0},{2,3},{3,2},{4,5},{5,4},{6,7},{7,6},{8,9},{9,8},{10,11... | collective-permute-start | bytes 1179656 | tf_op jit(solution)/shard_map/ppermute | solution.py:349
  76.6 10.7 %collective-permute-start.14 = (f32[1,1536]{1,0:T(1,128)S(1)}, f32[1,1536]{1,0:T(1,128)S(1)}, u32[]{:S(2)}, u32[]{:S(2)}) collective-permute-start(f32[1,1536]{1,0:T(1,128)S(1)} %reshape.236), channel_id=1, source_target_pairs={{0,1},{1,0},{2,3},{3,2},{4,5},{5,4},{6,7},{7,6},{8,9},{9,8},{10,11... | collective-permute-start | bytes 18440 | tf_op jit(solution)/shard_map/ppermute | solution.py:349
  78.1 50.3 %collective-permute-start.19 = (bf16[384,1536]{1,0:T(8,128)(2,1)}, bf16[384,1536]{1,0:T(8,128)(2,1)}, u32[]{:S(2)}, u32[]{:S(2)}) collective-permute-start(bf16[384,1536]{1,0:T(8,128)(2,1)} %constant_dynamic-update-slice_fusion.5.refs_7_), channel_id=1, source_target_pairs={{0,1},{1,0},{2,3},{3,2},{4,5},{5,4},{6,7},{7,6},{8,9},{9,8},{10,11... | collective-permute-start | bytes 3538952 | tf_op jit(solution)/shard_map/ppermute | solution.py:349
  78.7 38.3 %collective-permute-start.12 = (bf16[256,768]{1,0:T(8,128)(2,1)S(1)}, bf16[256,768]{1,0:T(8,128)(2,1)S(1)}, u32[]{:S(2)}, u32[]{:S(2)}) collective-permute-start(bf16[256,768]{1,0:T(8,128)(2,1)S(1)} %collective-permute-done.1.refs_0_.refs_7_), channel_id=1, source_target_pairs={{0,1},{1,0},{2,3},{3,2},{4,5},{5,4},{6,7},{7,6},{8,9},{9,8},{10,11... | collective-permute-start | bytes 1179656 | tf_op jit(solution)/shard_map/ppermute | solution.py:349
  87.4 39.3 %collective-permute-start.9 = (bf16[3,384,384]{2,1,0:T(8,128)(2,1)S(1)}, bf16[3,384,384]{2,1,0:T(8,128)(2,1)}, u32[]{:S(2)}, u32[]{:S(2)}) collective-permute-start(bf16[3,384,384]{2,1,0:T(8,128)(2,1)S(1)} %constant_dynamic-update-slice_fusion.refs_3_), channel_id=1, source_target_pairs={{0,16},{16,0},{1,17},{17,1},{2,18},{18,2},{3,19},{19,3},{4,20},{20... | collective-permute-start | bytes 2654216 | tf_op jit(solution)/shard_map/ppermute | solution.py:349
  89.1 38.9 %collective-permute-start.10 = (bf16[3,384,384]{2,1,0:T(8,128)(2,1)S(1)}, bf16[3,384,384]{2,1,0:T(8,128)(2,1)}, u32[]{:S(2)}, u32[]{:S(2)}) collective-permute-start(bf16[3,384,384]{2,1,0:T(8,128)(2,1)S(1)} %constant_dynamic-update-slice_fusion.refs_3_), channel_id=1, source_target_pairs={{0,8},{8,0},{1,9},{9,1},{2,10},{10,2},{3,11},{11,3},{4,12},{12,4},... | collective-permute-start | bytes 2654216 | tf_op jit(solution)/shard_map/ppermute | solution.py:349
  116.9 9.7 %collective-permute-start.2 = (bf16[256,768]{1,0:T(8,128)(2,1)S(1)}, bf16[256,768]{1,0:T(8,128)(2,1)}, u32[]{:S(2)}, u32[]{:S(2)}) collective-permute-start(bf16[256,768]{1,0:T(8,128)(2,1)S(1)} %collective-permute-done.1.refs_0_.refs_7_), channel_id=1, source_target_pairs={{0,2},{2,4},{4,6},{6,0},{1,3},{3,5},{5,7},{7,1},{8,10},{10,12},{12... | collective-permute-start | bytes 1179656 | tf_op jit(solution)/shard_map/ppermute | solution.py:345
  126.6 40.8 %collective-permute-start.27 = (bf16[384,1920]{1,0:T(8,128)(2,1)}, bf16[384,1920]{1,0:T(8,128)(2,1)}, u32[]{:S(2)}, u32[]{:S(2)}) collective-permute-start(bf16[384,1920]{1,0:T(8,128)(2,1)} %constant_dynamic-update-slice_fusion.12.refs_11_), channel_id=1, source_target_pairs={{0,8},{8,0},{1,9},{9,1},{2,10},{10,2},{3,11},{11,3},{4,12},{12,4},... | collective-permute-start | bytes 4423688 | tf_op jit(solution)/shard_map/ppermute | solution.py:349
  126.6 4.9 %collective-permute-start.11 = (bf16[3,384,384]{2,1,0:T(8,128)(2,1)}, bf16[3,384,384]{2,1,0:T(8,128)(2,1)}, u32[]{:S(2)}, u32[]{:S(2)}) collective-permute-start(bf16[3,384,384]{2,1,0:T(8,128)(2,1)} %collective-permute-done.9.refs_4_), channel_id=1, source_target_pairs={{0,8},{8,0},{1,9},{9,1},{2,10},{10,2},{3,11},{11,3},{4,12},{12,4},... | collective-permute-start | bytes 2654216 | tf_op jit(solution)/shard_map/ppermute | solution.py:349
  127.1 40.3 %collective-permute-start.28 = (bf16[384,1920]{1,0:T(8,128)(2,1)}, bf16[384,1920]{1,0:T(8,128)(2,1)}, u32[]{:S(2)}, u32[]{:S(2)}) collective-permute-start(bf16[384,1920]{1,0:T(8,128)(2,1)} %collective-permute-done.26.refs_12_), channel_id=1, source_target_pairs={{0,8},{8,0},{1,9},{9,1},{2,10},{10,2},{3,11},{11,3},{4,12},{12,4},... | collective-permute-start | bytes 4423688 | tf_op jit(solution)/shard_map/ppermute | solution.py:349
  128.0 39.4 %collective-permute-start.20 = (bf16[384,1536]{1,0:T(8,128)(2,1)}, bf16[384,1536]{1,0:T(8,128)(2,1)}, u32[]{:S(2)}, u32[]{:S(2)}) collective-permute-start(bf16[384,1536]{1,0:T(8,128)(2,1)} %constant_dynamic-update-slice_fusion.5.refs_7_), channel_id=1, source_target_pairs={{0,8},{8,0},{1,9},{9,1},{2,10},{10,2},{3,11},{11,3},{4,12},{12,4},... | collective-permute-start | bytes 3538952 | tf_op jit(solution)/shard_map/ppermute | solution.py:349
  128.4 39.0 %collective-permute-start.21 = (bf16[384,1536]{1,0:T(8,128)(2,1)}, bf16[384,1536]{1,0:T(8,128)(2,1)}, u32[]{:S(2)}, u32[]{:S(2)}) collective-permute-start(bf16[384,1536]{1,0:T(8,128)(2,1)} %collective-permute-done.19.refs_8_), channel_id=1, source_target_pairs={{0,8},{8,0},{1,9},{9,1},{2,10},{10,2},{3,11},{11,3},{4,12},{12,4},... | collective-permute-start | bytes 3538952 | tf_op jit(solution)/shard_map/ppermute | solution.py:349
  131.5 24.7 %collective-permute-start.3 = (bf16[256,768]{1,0:T(8,128)(2,1)}, bf16[256,768]{1,0:T(8,128)(2,1)S(1)}, u32[]{:S(2)}, u32[]{:S(2)}) collective-permute-start(bf16[256,768]{1,0:T(8,128)(2,1)} %collective-permute-done.2.refs_0_.refs_9_), channel_id=1, source_target_pairs={{0,1},{1,0},{2,3},{3,2},{4,5},{5,4},{6,7},{7,6},{8,9},{9,8},{10,11... | collective-permute-start | bytes 1179656 | tf_op jit(solution)/shard_map/ppermute | solution.py:349
  138.5 82.5 %copy-start.2 = (bf16[3,768,768]{2,1,0:T(8,128)(2,1)}, bf16[3,768,768]{2,1,0:T(8,128)(2,1)S(1)}, u32[]{:S(2)}) copy-start(bf16[3,768,768]{2,1,0:T(8,128)(2,1)S(1)} %get-tuple-element.81.refs_2_.refs_3_.refs_9_.refs_10_) | copy-start | bytes 10616836
  246.8 1.3 collective-permute-start.44
  248.8 4.3 collective-permute-start.45
  250.1 30.7 %collective-permute-start.31 = (bf16[256,768]{1,0:T(8,128)(2,1)}, bf16[256,768]{1,0:T(8,128)(2,1)}, u32[]{:S(2)}, u32[]{:S(2)}) collective-permute-start(bf16[256,768]{1,0:T(8,128)(2,1)} %copy-done.93), channel_id=1, source_target_pairs={{0,1},{1,0},{2,3},{3,2},{4,5},{5,4},{6,7},{7,6},{8,9},{9,8},{10,11... | collective-permute-start | bytes 1179656 | tf_op jit(solution)/shard_map/ppermute | solution.py:349
  253.9 4.1 collective-permute-start.46
  258.0 4.1 collective-permute-start.47
  262.8 15.9 %collective-permute-start.48 = (f32[84,128]{1,0:T(8,128)}, f32[84,128]{1,0:T(8,128)}, u32[]{:S(2)}, u32[]{:S(2)}) collective-permute-start(f32[84,128]{1,0:T(8,128)} %add.147), channel_id=1, source_target_pairs={{0,4},{2,6},{4,0},{6,2},{1,5},{3,7},{5,1},{7,3},{8,12},{10,14},{12... | collective-permute-start | bytes 129032 | tf_op jit(solution)/shard_map/ppermute | solution.py:406
  276.6 67.1 %collective-permute-start.55 = (bf16[2,2,192,1536]{3,2,1,0:T(8,128)(2,1)S(1)}, bf16[2,2,192,1536]{3,2,1,0:T(8,128)(2,1)S(1)}, u32[]{:S(2)}, u32[]{:S(2)}) collective-permute-start(bf16[2,2,192,1536]{3,2,1,0:T(8,128)(2,1)S(1)} %get-tuple-element.147), channel_id=1, source_target_pairs={{0,8},{8,0},{1,9},{9,1},{2,10},{10,2},{3,11},{11,3},{4,12},{12,4},... | collective-permute-start | bytes 7077896 | tf_op jit(solution)/shard_map/ppermute | solution.py:349
  276.7 66.0 %collective-permute-start.38 = (bf16[2,2,3,192,384]{4,3,2,1,0:T(8,128)(2,1)S(1)}, bf16[2,2,3,192,384]{4,3,2,1,0:T(8,128)(2,1)S(1)}, u32[]{:S(2)}, u32[]{:S(2)}) collective-permute-start(bf16[2,2,3,192,384]{4,3,2,1,0:T(8,128)(2,1)S(1)} %copy-done.117), channel_id=1, source_target_pairs={{0,8},{8,0},{1,9},{9,1},{2,10},{10,2},{3,11},{11,3},{4,12},{12,4},... | collective-permute-start | bytes 5308424 | tf_op jit(solution)/shard_map/ppermute | solution.py:349
  277.2 29.7 %collective-permute-start.30 = (bf16[256,768]{1,0:T(8,128)(2,1)S(1)}, bf16[256,768]{1,0:T(8,128)(2,1)S(1)}, u32[]{:S(2)}, u32[]{:S(2)}) collective-permute-start(bf16[256,768]{1,0:T(8,128)(2,1)S(1)} %copy-done.99), channel_id=1, source_target_pairs={{0,1},{1,0},{2,3},{3,2},{4,5},{5,4},{6,7},{7,6},{8,9},{9,8},{10,11... | collective-permute-start | bytes 1179656 | tf_op jit(solution)/shard_map/ppermute | solution.py:349
  278.7 18.9 %collective-permute-start.33 = (bf16[256,768]{1,0:T(8,128)(2,1)S(1)}, bf16[256,768]{1,0:T(8,128)(2,1)S(1)}, u32[]{:S(2)}, u32[]{:S(2)}) collective-permute-start(bf16[256,768]{1,0:T(8,128)(2,1)S(1)} %copy-done.95), channel_id=1, source_target_pairs={{0,1},{1,0},{2,3},{3,2},{4,5},{5,4},{6,7},{7,6},{8,9},{9,8},{10,11... | collective-permute-start | bytes 1179656 | tf_op jit(solution)/shard_map/ppermute | solution.py:349
  280.8 25.2 %collective-permute-start.35 = (bf16[256,768]{1,0:T(8,128)(2,1)S(1)}, bf16[256,768]{1,0:T(8,128)(2,1)S(1)}, u32[]{:S(2)}, u32[]{:S(2)}) collective-permute-start(bf16[256,768]{1,0:T(8,128)(2,1)S(1)} %copy-done.97), channel_id=1, source_target_pairs={{0,1},{1,0},{2,3},{3,2},{4,5},{5,4},{6,7},{7,6},{8,9},{9,8},{10,11... | collective-permute-start | bytes 1179656 | tf_op jit(solution)/shard_map/ppermute | solution.py:349
  297.6 16.0 %collective-permute-start.29 = (bf16[256,768]{1,0:T(8,128)(2,1)S(1)}, bf16[256,768]{1,0:T(8,128)(2,1)S(1)}, u32[]{:S(2)}, u32[]{:S(2)}) collective-permute-start(bf16[256,768]{1,0:T(8,128)(2,1)S(1)} %copy-done.109), channel_id=1, source_target_pairs={{0,1},{1,0},{2,3},{3,2},{4,5},{5,4},{6,7},{7,6},{8,9},{9,8},{10,11... | collective-permute-start | bytes 1179656 | tf_op jit(solution)/shard_map/ppermute | solution.py:349
  306.0 10.5 %collective-permute-start.32 = (bf16[256,768]{1,0:T(8,128)(2,1)S(1)}, bf16[256,768]{1,0:T(8,128)(2,1)S(1)}, u32[]{:S(2)}, u32[]{:S(2)}) collective-permute-start(bf16[256,768]{1,0:T(8,128)(2,1)S(1)} %add_convert_fusion.3), channel_id=1, source_target_pairs={{0,6},{2,0},{4,2},{6,4},{1,7},{3,1},{5,3},{7,5},{8,14},{10,8},{12,... | collective-permute-start | bytes 1179656 | tf_op jit(solution)/shard_map/ppermute | solution.py:345
  306.9 33.8 %collective-permute-start.34 = (bf16[256,768]{1,0:T(8,128)(2,1)S(1)}, bf16[256,768]{1,0:T(8,128)(2,1)S(1)}, u32[]{:S(2)}, u32[]{:S(2)}) collective-permute-start(bf16[256,768]{1,0:T(8,128)(2,1)S(1)} %add_convert_fusion.2), channel_id=1, source_target_pairs={{0,4},{2,6},{4,0},{6,2},{1,5},{3,7},{5,1},{7,3},{8,12},{10,14},{12... | collective-permute-start | bytes 1179656 | tf_op jit(solution)/shard_map/ppermute | solution.py:345
  313.6 27.2 %collective-permute-start.36 = (bf16[256,768]{1,0:T(8,128)(2,1)S(1)}, bf16[256,768]{1,0:T(8,128)(2,1)S(1)}, u32[]{:S(2)}, u32[]{:S(2)}) collective-permute-start(bf16[256,768]{1,0:T(8,128)(2,1)S(1)} %add_convert_fusion.1), channel_id=1, source_target_pairs={{0,2},{2,4},{4,6},{6,0},{1,3},{3,5},{5,7},{7,1},{8,10},{10,12},{12... | collective-permute-start | bytes 1179656 | tf_op jit(solution)/shard_map/ppermute | solution.py:345
  316.5 50.7 %collective-permute-start.49 = (bf16[2,2,192,1920]{3,2,1,0:T(8,128)(2,1)}, bf16[2,2,192,1920]{3,2,1,0:T(8,128)(2,1)S(1)}, u32[]{:S(2)}, u32[]{:S(2)}) collective-permute-start(bf16[2,2,192,1920]{3,2,1,0:T(8,128)(2,1)} %get-tuple-element.145), channel_id=1, source_target_pairs={{0,8},{8,0},{1,9},{9,1},{2,10},{10,2},{3,11},{11,3},{4,12},{12,4},... | collective-permute-start | bytes 8847368 | tf_op jit(solution)/shard_map/ppermute | solution.py:349
  341.1 40.0 %collective-permute-start.37 = (bf16[256,768]{1,0:T(8,128)(2,1)S(1)}, bf16[256,768]{1,0:T(8,128)(2,1)S(1)}, u32[]{:S(2)}, u32[]{:S(2)}) collective-permute-start(bf16[256,768]{1,0:T(8,128)(2,1)S(1)} %add_convert_fusion), channel_id=1, source_target_pairs={{0,1},{1,0},{2,3},{3,2},{4,5},{5,4},{6,7},{7,6},{8,9},{9,8},{10,11... | collective-permute-start | bytes 1179656 | tf_op jit(solution)/shard_map/ppermute | solution.py:349
  343.2 22.6 %collective-permute-start.39 = (bf16[2,3,192,384]{3,2,1,0:T(8,128)(2,1)S(1)}, bf16[2,3,192,384]{3,2,1,0:T(8,128)(2,1)S(1)}, u32[]{:S(2)}, u32[]{:S(2)}) collective-permute-start(bf16[2,3,192,384]{3,2,1,0:T(8,128)(2,1)S(1)} %fusion.8), channel_id=1, source_target_pairs={{0,16},{16,0},{1,17},{17,1},{2,18},{18,2},{3,19},{19,3},{4,20},{20... | collective-permute-start | bytes 2654216 | tf_op jit(solution)/shard_map/ppermute | solution.py:349
  344.5 43.9 %collective-permute-start.56 = (bf16[2,192,1536]{2,1,0:T(8,128)(2,1)S(1)}, bf16[2,192,1536]{2,1,0:T(8,128)(2,1)S(1)}, u32[]{:S(2)}, u32[]{:S(2)}) collective-permute-start(bf16[2,192,1536]{2,1,0:T(8,128)(2,1)S(1)} %fusion.5), channel_id=1, source_target_pairs={{0,16},{16,0},{1,17},{17,1},{2,18},{18,2},{3,19},{19,3},{4,20},{20... | collective-permute-start | bytes 3538952 | tf_op jit(solution)/shard_map/ppermute | solution.py:349
  366.1 13.2 %collective-permute-start.40 = (bf16[3,192,384]{2,1,0:T(8,128)(2,1)S(1)}, bf16[3,192,384]{2,1,0:T(8,128)(2,1)S(1)}, u32[]{:S(2)}, u32[]{:S(2)}) collective-permute-start(bf16[3,192,384]{2,1,0:T(8,128)(2,1)S(1)} %fusion.13), channel_id=1, source_target_pairs={{0,1},{1,0},{2,3},{3,2},{4,5},{5,4},{6,7},{7,6},{8,9},{9,8},{10,11... | collective-permute-start | bytes 1327112 | tf_op jit(solution)/shard_map/ppermute | solution.py:349
  367.9 40.6 %collective-permute-start.50 = (bf16[2,192,1920]{2,1,0:T(8,128)(2,1)S(1)}, bf16[2,192,1920]{2,1,0:T(8,128)(2,1)S(1)}, u32[]{:S(2)}, u32[]{:S(2)}) collective-permute-start(bf16[2,192,1920]{2,1,0:T(8,128)(2,1)S(1)} %fusion.3), channel_id=1, source_target_pairs={{0,1},{1,0},{2,3},{3,2},{4,5},{5,4},{6,7},{7,6},{8,9},{9,8},{10,11... | collective-permute-start | bytes 4423688 | tf_op jit(solution)/shard_map/ppermute | solution.py:349
  379.4 6.0 %collective-permute-start.41 = (bf16[3,48,384]{2,1,0:T(8,128)(2,1)S(1)}, bf16[3,48,384]{2,1,0:T(8,128)(2,1)S(1)}, u32[]{:S(2)}, u32[]{:S(2)}) collective-permute-start(bf16[3,48,384]{2,1,0:T(8,128)(2,1)S(1)} %get-tuple-element.166), channel_id=1, source_target_pairs={{0,6},{2,0},{4,2},{6,4},{1,7},{3,1},{5,3},{7,5},{8,14},{10,8},{12,... | collective-permute-start | bytes 331784 | tf_op jit(solution)/shard_map/ppermute | solution.py:345
  379.5 5.9 %collective-permute-start.42 = (bf16[3,48,384]{2,1,0:T(8,128)(2,1)S(1)}, bf16[3,48,384]{2,1,0:T(8,128)(2,1)S(1)}, u32[]{:S(2)}, u32[]{:S(2)}) collective-permute-start(bf16[3,48,384]{2,1,0:T(8,128)(2,1)S(1)} %get-tuple-element.168), channel_id=1, source_target_pairs={{0,4},{2,6},{4,0},{6,2},{1,5},{3,7},{5,1},{7,3},{8,12},{10,14},{12... | collective-permute-start | bytes 331784 | tf_op jit(solution)/shard_map/ppermute | solution.py:345
  381.1 6.6 %collective-permute-start.43 = (bf16[3,48,384]{2,1,0:T(8,128)(2,1)S(1)}, bf16[3,48,384]{2,1,0:T(8,128)(2,1)S(1)}, u32[]{:S(2)}, u32[]{:S(2)}) collective-permute-start(bf16[3,48,384]{2,1,0:T(8,128)(2,1)S(1)} %get-tuple-element.167), channel_id=1, source_target_pairs={{0,2},{2,4},{4,6},{6,0},{1,3},{3,5},{5,7},{7,1},{8,10},{10,12},{12... | collective-permute-start | bytes 331784 | tf_op jit(solution)/shard_map/ppermute | solution.py:345
  388.9 26.0 %collective-permute-start.57 = (bf16[192,1536]{1,0:T(8,128)(2,1)S(1)}, bf16[192,1536]{1,0:T(8,128)(2,1)S(1)}, u32[]{:S(2)}, u32[]{:S(2)}) collective-permute-start(bf16[192,1536]{1,0:T(8,128)(2,1)S(1)} %fusion.12), channel_id=1, source_target_pairs={{0,1},{1,0},{2,3},{3,2},{4,5},{5,4},{6,7},{7,6},{8,9},{9,8},{10,11... | collective-permute-start | bytes 1769480 | tf_op jit(solution)/shard_map/ppermute | solution.py:349
  408.9 15.0 %collective-permute-start.51 = (bf16[192,1920]{1,0:T(8,128)(2,1)S(1)}, bf16[192,1920]{1,0:T(8,128)(2,1)S(1)}, u32[]{:S(2)}, u32[]{:S(2)}) collective-permute-start(bf16[192,1920]{1,0:T(8,128)(2,1)S(1)} %fusion.11), channel_id=1, source_target_pairs={{0,16},{16,0},{1,17},{17,1},{2,18},{18,2},{3,19},{19,3},{4,20},{20... | collective-permute-start | bytes 2211848 | tf_op jit(solution)/shard_map/ppermute | solution.py:349
  415.0 11.9 %collective-permute-start.58 = (bf16[48,1536]{1,0:T(8,128)(2,1)S(1)}, bf16[48,1536]{1,0:T(8,128)(2,1)S(1)}, u32[]{:S(2)}, u32[]{:S(2)}) collective-permute-start(bf16[48,1536]{1,0:T(8,128)(2,1)S(1)} %get-tuple-element.159), channel_id=1, source_target_pairs={{0,6},{2,0},{4,2},{6,4},{1,7},{3,1},{5,3},{7,5},{8,14},{10,8},{12,... | collective-permute-start | bytes 442376 | tf_op jit(solution)/shard_map/ppermute | solution.py:345
  415.1 27.8 %collective-permute-start.59 = (bf16[48,1536]{1,0:T(8,128)(2,1)S(1)}, bf16[48,1536]{1,0:T(8,128)(2,1)S(1)}, u32[]{:S(2)}, u32[]{:S(2)}) collective-permute-start(bf16[48,1536]{1,0:T(8,128)(2,1)S(1)} %get-tuple-element.161), channel_id=1, source_target_pairs={{0,4},{2,6},{4,0},{6,2},{1,5},{3,7},{5,1},{7,3},{8,12},{10,14},{12... | collective-permute-start | bytes 442376 | tf_op jit(solution)/shard_map/ppermute | solution.py:345
  422.0 20.9 %collective-permute-start.60 = (bf16[48,1536]{1,0:T(8,128)(2,1)S(1)}, bf16[48,1536]{1,0:T(8,128)(2,1)S(1)}, u32[]{:S(2)}, u32[]{:S(2)}) collective-permute-start(bf16[48,1536]{1,0:T(8,128)(2,1)S(1)} %get-tuple-element.160), channel_id=1, source_target_pairs={{0,2},{2,4},{4,6},{6,0},{1,3},{3,5},{5,7},{7,1},{8,10},{10,12},{12... | collective-permute-start | bytes 442376 | tf_op jit(solution)/shard_map/ppermute | solution.py:345
  424.2 19.5 %collective-permute-start.52 = (bf16[48,1920]{1,0:T(8,128)(2,1)S(1)}, bf16[48,1920]{1,0:T(8,128)(2,1)S(1)}, u32[]{:S(2)}, u32[]{:S(2)}) collective-permute-start(bf16[48,1920]{1,0:T(8,128)(2,1)S(1)} %get-tuple-element.156), channel_id=1, source_target_pairs={{0,6},{2,0},{4,2},{6,4},{1,7},{3,1},{5,3},{7,5},{8,14},{10,8},{12,... | collective-permute-start | bytes 552968 | tf_op jit(solution)/shard_map/ppermute | solution.py:345
  426.1 21.8 %collective-permute-start.53 = (bf16[48,1920]{1,0:T(8,128)(2,1)S(1)}, bf16[48,1920]{1,0:T(8,128)(2,1)S(1)}, u32[]{:S(2)}, u32[]{:S(2)}) collective-permute-start(bf16[48,1920]{1,0:T(8,128)(2,1)S(1)} %get-tuple-element.158), channel_id=1, source_target_pairs={{0,4},{2,6},{4,0},{6,2},{1,5},{3,7},{5,1},{7,3},{8,12},{10,14},{12... | collective-permute-start | bytes 552968 | tf_op jit(solution)/shard_map/ppermute | solution.py:345
  426.9 21.0 %collective-permute-start.54 = (bf16[48,1920]{1,0:T(8,128)(2,1)S(1)}, bf16[48,1920]{1,0:T(8,128)(2,1)S(1)}, u32[]{:S(2)}, u32[]{:S(2)}) collective-permute-start(bf16[48,1920]{1,0:T(8,128)(2,1)S(1)} %get-tuple-element.157), channel_id=1, source_target_pairs={{0,2},{2,4},{4,6},{6,0},{1,3},{3,5},{5,7},{7,1},{8,10},{10,12},{12... | collective-permute-start | bytes 552968 | tf_op jit(solution)/shard_map/ppermute | solution.py:345
  (115 other events, 1451.4 us)
